TPU v7x, 256 devices: a whole 4x4x8 slice. The times are simulated.
256 devices in a mesh: fit: 8 (over z_hi, x), pair: 16 (over y, z_lo), blk: 2 (over core).
Axes of the slice: x: 4, y: 4, z: 8 (z_hi: 2, z_lo: 4; z = z_hi * 4 + z_lo), core: 2. Of those that a mesh axis runs over, the one named last changes fastest.
Arguments:
- left_factor: float32 [128, 512, 2048], P('pair', 'blk', 'fit'), may hold values from -2 to 2
- right_factor: float32 [128, 512, 2048], P('pair', None, 'fit'), may hold values from -2 to 2
- amplitudes: float32 [128, 512, 512], P(('pair', 'fit'), 'blk'), may hold values from -6 to 6
- domain_trans: float32 [128, 512, 512], P(('pair', 'fit')), may hold values from -0.25 to 0.25
- vir_energy: float32 [128, 512], P(('pair', 'fit')), may hold values from 0.5 to 3
- occ_energy: float32 [128], P(('pair', 'fit')), may hold values from 0.2 to 1
- coupling: float32 [128, 4], P(('pair', 'fit')), may hold values from -4 to 4
- neighbours: int32 [128, 4], P(('pair', 'fit')), may hold values from 0 to 127, as said below
- dom_blocks: int32 [128], P(('pair', 'fit')), may hold values from 1 to 4
Outputs:
- new_amplitudes: float32 [128, 512, 512], P(('pair', 'fit'), 'blk')
- density_fit: float32 [128, 2048], P('pair', 'fit')
Inputs may be any that keep to these rules, and one draw needn't show every extreme that they name: `neighbours`: with s(p) = p // 8, each entry names a pair p' with (p') % 8 equal to that of the listing pair p, and s(p') equal to s(p), s(p) + 1, s(p) - 1 or s(p) + 8, modulo 16; entries may repeat.
All inputs are finite; a program needn't handle non-finite values.
Results may differ from a plain program's by a relative error of at most 0.000068.
Values sent between devices are 32-bit elements; how exact they have to be, the bound alone decides.
No kernel may reach another device: no remote copies, remote signals or barrier semaphores. Data moves between devices by JAX's collectives and lax.ppermute only.
A program may use at most 64 MiB of HBM per device.

v0:
```python
import functools

import jax
import jax.numpy as jnp
from jax import lax
from jax.experimental import pallas as pl
from jax.experimental.pallas import tpu as pltpu
from jax.sharding import PartitionSpec as P


F32 = jnp.float32
NT = (((1,), (1,)), ((), ()))
NN = (((1,), (0,)), ((), ()))
ANY = pl.BlockSpec(memory_space=pltpu.HBM)
SCALARS = pl.BlockSpec(memory_space=pltpu.SMEM)
WHOLE = pl.BlockSpec(memory_space=pltpu.VMEM)
LIMIT = pltpu.CompilerParams(vmem_limit_bytes=16 << 20)
SEGMENT = 4
EXTRA = 8


def halves(v):
    top = v.astype(jnp.bfloat16)
    return top, (v - top.astype(F32)).astype(jnp.bfloat16)


def dot3(a, b, dims):
    a_top, a_low = a
    b_top, b_low = b
    dot = functools.partial(lax.dot_general, dimension_numbers=dims, preferred_element_type=F32)
    return (dot(a_low, b_top) + dot(a_top, b_low)) + dot(a_top, b_top)


def seat(ring, own):
    fit = lax.axis_index("fit")
    side = fit // ring
    return fit % ring, (side if own else 1 - side) * ring


def fill_packs(ring, own, left, right, outs, sems):
    place, first = seat(ring, own)
    rows = left.shape[1]
    half = right.shape[1] // 2
    part = half // 2
    start = lax.axis_index("blk") * half
    copies = []
    for by in range(1, ring):
        slot = first + (place + by) % ring
        long, short = outs[by - 1], outs[ring - 2 + by]
        for i, (source, to) in enumerate((
            (left.at[slot], long.at[0:rows]),
            (right.at[slot, pl.ds(pl.multiple_of(start, part), part)], long.at[rows : rows + part]),
            (right.at[slot, pl.ds(pl.multiple_of(start + part, part), part)], short),
        )):
            copies.append(pltpu.make_async_copy(source, to, sems.at[by - 1, i]))
    for copy in copies:
        copy.start()
    return copies


def pack_kernel(ring, own, left, right, _, *refs):
    for copy in fill_packs(ring, own, left, right, refs[:-1], refs[-1]):
        copy.wait()


def head_kernel(ring, left, right, amp, trans, *refs):
    *packs, mixed, amp_here, trans_here, sems, own_sems = refs
    reads = [
        pltpu.make_async_copy(amp, amp_here, own_sems.at[0]),
        pltpu.make_async_copy(trans, trans_here, own_sems.at[1]),
    ]
    for read in reads:
        read.start()
    copies = fill_packs(ring, False, left, right, packs, sems)
    for read in reads:
        read.wait()
    mixed[...] = dot3(halves(amp_here[...]), halves(trans_here[...]), NT)
    for copy in copies:
        copy.wait()


def gather_kernel(*refs):
    *sources, out_ref = refs
    part = out_ref.shape[1]
    for i, source in enumerate(sources):
        out_ref[i] = source[source.shape[0] - part :, :]


def fetch(ring, own, left, right, left_here, right_here, sems):
    place, first = seat(ring, own)
    copies = [
        pltpu.make_async_copy(left.at[first + place], left_here, sems.at[0]),
        pltpu.make_async_copy(right.at[first + place], right_here, sems.at[1]),
    ]
    for copy in copies:
        copy.start()
    return copies


def columns(part, which):
    core = lax.axis_index("blk")
    return [pl.ds(pl.multiple_of((2 * c + which) * part, part), part) for c in (core, 1 - core)]


def integral_kernel(ring, own, which, left, right, *refs):
    (*packs, rights, out_ref, left_here, right_here, sems) = refs
    copies = fetch(ring, own, left, right, left_here, right_here, sems)
    rows = left_here.shape[0]
    part = rights.shape[1]
    total = None
    for i, pack in enumerate(packs):
        term = dot3(halves(pack[0:rows, :]), halves(rights[i]), NT)
        total = term if total is None else total + term
    for copy in copies:
        copy.wait()
    own_left = halves(left_here[...])
    mine, yours = columns(part, which)
    out_ref[:, 0:part] = total + dot3(own_left, halves(right_here[mine, :]), NT)
    out_ref[:, part:] = dot3(own_left, halves(right_here[yours, :]), NT)


def finished(part_ref, packs, others):
    rows, part = part_ref.shape[0], others.shape[1]
    total = part_ref[:, part:]
    for i, pack in enumerate(packs):
        total += dot3(halves(pack[0:rows, :]), halves(others[i]), NT)
    return jnp.concatenate([part_ref[:, 0:part], total], axis=1)


def finish_kernel(part_ref, *refs):
    *packs, others, out_ref = refs
    out_ref[...] = finished(part_ref, packs, others)


def denominators(facts, rows):
    width = facts.shape[1]
    column = jnp.broadcast_to(facts[1:2, 0:rows], (128, rows)).T
    return jnp.concatenate([column] * (width // 128), axis=1) + facts[0:1, :] + facts[2:3, 0:1]


def residual_kernel(which, occ, dom, part_ref, *refs):
    *packs, others, amp, corr, vir, out_ref = refs
    rows, width = amp.shape
    part = others.shape[1]
    spots = columns(part, which)
    core = lax.axis_index("blk")
    out_ref[rows:, :] = jnp.concatenate([
        jnp.concatenate([vir[:, spot] for spot in spots], axis=1),
        vir[:, pl.ds(pl.multiple_of(core * rows, rows), rows)],
        jnp.full((1, 2 * part), occ[0], F32),
        jnp.full((1, 2 * part), (dom[0] * (width // 4)).astype(F32), F32),
        jnp.zeros((EXTRA - 4, 2 * part), F32),
    ])
    below = denominators(out_ref.at[rows : rows + EXTRA], rows)
    old = jnp.concatenate([amp[:, spot] for spot in spots], axis=1)
    fixed = below * old - jnp.concatenate([corr[:, spot] for spot in spots], axis=1)
    residual = finished(part_ref, packs, others) + fixed
    out_ref[0:rows, :] = old - 0.7 * residual / below


def density_kernel(ring, own, which, left, right, *refs):
    refs = list(refs)
    take = lambda n: [refs.pop(0) for _ in range(n)]
    longs = take(ring - 1)
    shorts = take(ring - 1) if 1 in which else []
    others = dict(zip(which, take(len(which))))
    early, late = take(len(which)), take(len(which))
    before = None if 0 in which else take(1)[0]
    new_ref = take(1)[0] if own else None
    sums_ref, left_here, right_here, sems = refs
    copies = fetch(ring, own, left, right, left_here, right_here, sems)
    rows, part = late[0].shape[0], late[0].shape[1] // 2
    core = lax.axis_index("blk")
    row = (core * rows + lax.broadcasted_iota(jnp.int32, (rows, 2 * part), 0)).astype(F32)
    lane = lax.broadcasted_iota(jnp.int32, (rows, 2 * part), 1)
    new = {}
    for w, block, term in zip(which, early, late):
        facts = block.at[rows : rows + EXTRA]
        below = denominators(facts, rows)
        offset = jnp.where(lane < part, 2 * core * part, (1 - 2 * core) * part) + w * part
        column = (lane + offset).astype(F32)
        limit = facts[3:4, 0:1]
        updated = block[0:rows, :] - 0.7 * term[...] / below
        value = jnp.where((row < limit) & (column < limit), updated, 0.0)
        if own:
            mine, yours = columns(part, w)
            new_ref[:, mine] = value[:, 0:part]
            new_ref[:, yours] = value[:, part:]
        new[w] = halves(value)

    def add_up(spot, lefts, rights):
        product = None
        for w, value in new.items():
            term = dot3(value, halves(rights(w)), NN)
            product = term if product is None else product + term
        sums_ref[spot : spot + 1, :] = jnp.sum(lefts * product, axis=0, keepdims=True)

    for i, long in enumerate(longs):
        add_up(
            i + 1,
            long[0:rows, :],
            lambda w: jnp.concatenate([long[rows:, :] if w == 0 else shorts[i][...], others[w][i]], axis=0),
        )
    for copy in copies:
        copy.wait()
    add_up(0, left_here[...], lambda w: jnp.concatenate([right_here[spot, :] for spot in columns(part, w)], axis=0))
    if before is not None:
        sums_ref[...] += before[...]


def correction_kernel(pairs_per_shard, shards, neighbours, coupling, mixed, up, down, wrap, far, d_ref, out_ref):
    shard = lax.axis_index("pair")

    def weight(by):
        total = jnp.float32(0)
        for k in range(neighbours.shape[0]):
            apart = (neighbours[k] // pairs_per_shard - shard + shards) % shards
            total += jnp.where(apart == by, coupling[k], 0.0)
        return total

    above, below = weight(1), weight(shards - 1)
    spot = shard % SEGMENT
    ends = jnp.where(spot == SEGMENT - 1, above, jnp.where(spot == 0, below, 0.0))
    total = weight(0) * mixed[...] + above * up[...] + below * down[...]
    total += ends * wrap[...] + weight(shards // 2) * far[...]
    out_ref[...] = dot3(halves(total), halves(d_ref[...]), NN)


def vmem(*arrays):
    return [pltpu.with_memory_space_constraint(a, pltpu.VMEM) for a in arrays]


def hbm(*arrays):
    return [pltpu.with_memory_space_constraint(a, pltpu.HBM) for a in arrays]


def cost(flops, moved):
    return pl.CostEstimate(flops=flops, bytes_accessed=moved, transcendentals=0)


def body(left, right, amplitudes, domain_trans, vir_energy, occ_energy, coupling, neighbours, dom_blocks):
    fit_count, pair_count = lax.axis_size("fit"), lax.axis_size("pair")
    ring = fit_count // 2
    rows, width, depth = left.shape[1], right.shape[1], left.shape[2]
    fit = lax.axis_index("fit")
    side, place = fit // ring, fit % ring
    amp, trans = amplitudes[0], domain_trans[0]
    swap = [(0, 1), (1, 0)]
    across = [(f, (f + ring) % fit_count) for f in range(fit_count)]
    block = jax.ShapeDtypeStruct((rows, width), F32)
    sums = jax.ShapeDtypeStruct((ring, depth), F32)

    def shifted(by):
        return [(s * ring + i, s * ring + (i + by) % ring) for s in range(2) for i in range(ring)]

    def send(value, axis, pairs):
        return lax.ppermute(value, axis, pairs)

    def from_shards(value, sources):
        return send(value, "pair", [(source % pair_count, to) for to, source in sources])

    part = width // 4
    packs = [jax.ShapeDtypeStruct((rows + part, depth), F32)] * (ring - 1) + [jax.ShapeDtypeStruct((part, depth), F32)] * (ring - 1)
    pack_sems = pltpu.SemaphoreType.DMA((ring - 1, 3))
    some = jax.ShapeDtypeStruct((rows, 2 * part), F32)
    some_long = jax.ShapeDtypeStruct((rows + EXTRA, 2 * part), F32)
    edge = jax.ShapeDtypeStruct((ring - 1, part, depth), F32)

    def spread(values):
        return [send(value, "fit", shifted(by)) for by, value in enumerate(values, 1)]

    def swapped(values):
        gathered = pl.pallas_call(
            gather_kernel,
            in_specs=[WHOLE] * len(values),
            out_specs=WHOLE,
            out_shape=edge,
            compiler_params=LIMIT,
            cost_estimate=cost(0, 8 * edge.size),
        )(*vmem(*values))
        return gathered, send(gathered, "blk", swap)

    def work(kernel, own, which, factors, extras, outs):
        return pl.pallas_call(
            functools.partial(kernel, ring, own, which),
            in_specs=[ANY] * 2 + [WHOLE] * (len(factors) + len(extras)),
            out_specs=[WHOLE] * len(outs),
            out_shape=outs,
            scratch_shapes=[
                pltpu.VMEM((rows, depth), F32),
                pltpu.VMEM((width, depth), F32),
                pltpu.SemaphoreType.DMA((2,)),
            ],
            compiler_params=LIMIT,
            cost_estimate=cost(3 * rows * width * depth * ring, 2 * ring * depth * (rows + width)),
        )(*hbm(left, right), *vmem(*factors, *extras))

    *sent, mixed = pl.pallas_call(
        functools.partial(head_kernel, ring),
        in_specs=[ANY] * 4,
        out_specs=[WHOLE] * (2 * ring - 1),
        out_shape=packs + [block],
        scratch_shapes=[pltpu.VMEM(amp.shape, F32), pltpu.VMEM(trans.shape, F32), pack_sems, pltpu.SemaphoreType.DMA((2,))],
        compiler_params=LIMIT,
        cost_estimate=cost(6 * rows * width * width, 32 * rows * width),
    )(*hbm(left, right, amp, trans))
    their_longs, their_shorts = spread(sent[: ring - 1]), spread(sent[ring - 1 :])
    shards = range(pair_count)
    near = [
        from_shards(mixed, [(s, s + 1) for s in shards if s % SEGMENT < SEGMENT - 1]),
        from_shards(mixed, [(s, s - 1) for s in shards if s % SEGMENT > 0]),
        from_shards(mixed, [(s, s + 1) for s in shards if s % SEGMENT == SEGMENT - 1] + [(s, s - 1) for s in shards if s % SEGMENT == 0]),
        from_shards(mixed, [(s, s + pair_count // 2) for s in shards]),
    ]
    sent = pl.pallas_call(
        functools.partial(pack_kernel, ring, True),
        in_specs=[ANY] * 3,
        out_specs=[WHOLE] * len(packs),
        out_shape=packs,
        scratch_shapes=[pack_sems],
        compiler_params=LIMIT,
        cost_estimate=cost(0, 24 * rows * width),
    )(*hbm(left, right), mixed)
    my_longs, my_shorts = spread(sent[: ring - 1]), spread(sent[ring - 1 :])
    (corr,) = pl.pallas_call(
        functools.partial(correction_kernel, fit_count, pair_count),
        in_specs=[SCALARS] * 2 + [WHOLE] * 6,
        out_specs=[WHOLE],
        out_shape=[block],
        compiler_params=LIMIT,
        cost_estimate=cost(6 * rows * width * width, 28 * rows * width),
    )(neighbours[0], coupling[0], mixed, *near, trans)

    their_others, their_parts, my_late = [], [], []
    for which, source in enumerate((their_longs, their_shorts)):
        gathered, other = swapped(source)
        (started,) = work(integral_kernel, False, which, (*their_longs, gathered), (), [some])
        done = pl.pallas_call(
            finish_kernel,
            in_specs=[WHOLE] * (2 + len(their_longs)),
            out_specs=WHOLE,
            out_shape=some,
            compiler_params=LIMIT,
            cost_estimate=cost(2 * rows * width * depth, 16 * rows * width),
        )(started, *vmem(*their_longs, other))
        their_others.append(other)
        their_parts.append(done)
        my_late.append(send(done, "fit", across))
    my_others, my_early, their_early = [], [], []
    for which, source in enumerate((my_longs, my_shorts)):
        gathered, other = swapped(source)
        (started,) = work(integral_kernel, True, which, (*my_longs, gathered), (), [some])
        done = pl.pallas_call(
            functools.partial(residual_kernel, which),
            in_specs=[SCALARS] * 2 + [WHOLE] * (5 + len(my_longs)),
            out_specs=WHOLE,
            out_shape=some_long,
            compiler_params=LIMIT,
            cost_estimate=cost(2 * rows * width * depth, 24 * rows * width),
        )(occ_energy, dom_blocks, started, *vmem(*my_longs, other), amp, corr, vir_energy)
        my_others.append(other)
        my_early.append(done)
        their_early.append(send(done, "fit", across))
    new, my_sums = work(
        density_kernel, True, (0, 1), (*my_longs, *my_shorts, *my_others), (*my_early, *my_late), [block, sums]
    )
    (their_sums,) = work(
        density_kernel, False, (0,), (*their_longs, their_others[0]), (their_early[0], their_parts[0]), [sums]
    )
    (their_sums,) = work(
        density_kernel, False, (1,), (*their_longs, *their_shorts, their_others[1]),
        (their_early[1], their_parts[1], their_sums), [sums],
    )
    both = jnp.stack([my_sums, their_sums], axis=1)
    both = both + lax.ppermute(both, "blk", swap)
    parts = [both[0]] + [lax.ppermute(both[by], "fit", shifted(-by)) for by in range(1, ring)]
    density = jnp.zeros((2, ring, depth), F32)
    for by, part in enumerate(parts):
        at = (place + by) % ring
        density = jnp.where((jnp.arange(ring) == at)[None, :, None], part[:, None, :], density)
    density = jnp.where(side == 0, density, density[::-1])
    return new[None], density.reshape(fit_count, depth)


def solution(mesh):
    placed = (
        P("pair", "blk", "fit"),
        P("pair", None, "fit"),
        P(("pair", "fit"), "blk", None),
        P(("pair", "fit"), None, None),
        P(("pair", "fit"), None),
        P(("pair", "fit")),
        P(("pair", "fit"), None),
        P(("pair", "fit"), None),
        P(("pair", "fit")),
    )
    return jax.shard_map(
        lambda *args: body(*args),
        mesh=mesh,
        in_specs=placed,
        out_specs=(P(("pair", "fit"), "blk", None), P("pair", "fit")),
        check_vma=False,
    )
```

profile of v0, /device:TPU:1, one launch (start us, length us, event | category | flops | bytes accessed | tf_op | source)
XLA Modules:
  0.0 147.4 jit_solution(4604187089579619993)
XLA Ops:
  0.6 2.6 %shard_map.104 = (f32[384,256]{1,0:T(8,128)S(1)}, f32[384,256]{1,0:T(8,128)S(1)}, f32[384,256]{1,0:T(8,128)S(1)}, f32[128,256]{1,0:T(8,128)S(1)}, f32[128,256]{1...) custom-call(f32[8,256,256]{2,1,0:T(8,128)} %left.17, f32[8,512,256]{2,1,0:T(8,128)} %right.17, ...), custom_call_target="tpu_custom_call" | custom-call | flops 402653184 | bytes 4194304 | tf_op jit(solution)/shard_map/pallas_call | solution.py:298
  4.8 2.1 %collective-permute-start.3 = (f32[128,256]{1,0:T(8,128)S(1)}, f32[128,256]{1,0:T(8,128)S(1)}, u32[]{:S(2)}, u32[]{:S(2)}) collective-permute-start(f32[128,256]{1,0:T(8,128)S(1)} %get-tuple-element.21), channel_id=1, source_target_pairs={{0,32},{32,64},{64,96},{96,0},{128,160},{160,192},{192,224},{224,1... | collective-permute-start | bytes 393224 | tf_op jit(solution)/shard_map/ppermute | solution.py:257
  6.9 2.4 %collective-permute-start.4 = (f32[128,256]{1,0:T(8,128)S(1)}, f32[128,256]{1,0:T(8,128)S(1)}, u32[]{:S(2)}, u32[]{:S(2)}) collective-permute-start(f32[128,256]{1,0:T(8,128)S(1)} %get-tuple-element.22), channel_id=1, source_target_pairs={{0,64},{32,96},{64,0},{96,32},{128,192},{160,224},{192,128},{224,1... | collective-permute-start | bytes 393224 | tf_op jit(solution)/shard_map/ppermute | solution.py:257
  9.3 2.3 %collective-permute-start.13 = (f32[384,256]{1,0:T(8,128)S(1)}, f32[384,256]{1,0:T(8,128)S(1)}, u32[]{:S(2)}, u32[]{:S(2)}) collective-permute-start(f32[384,256]{1,0:T(8,128)S(1)} %get-tuple-element.25), channel_id=1, source_target_pairs={{0,64},{32,96},{64,0},{96,32},{128,192},{160,224},{192,128},{224,1... | collective-permute-start | bytes 1179656 | tf_op jit(solution)/shard_map/ppermute | solution.py:257
  13.1 1.9 %collective-permute-done.4.refs_1_.refs_4_ = f32[128,256]{1,0:T(8,128)S(1)} collective-permute-done((f32[128,256]{1,0:T(8,128)S(1)}, f32[128,256]{1,0:T(8,128)S(1)}, u32[]{:S(2)}, u32[]{:S(2)}) %collective-permute-start.4) | collective-permute-done | bytes 131104 | tf_op jit(solution)/shard_map/ppermute | solution.py:257
  15.7 9.5 %collective-permute-done.5.refs_2_.refs_5_ = f32[128,256]{1,0:T(8,128)S(1)} collective-permute-done((f32[128,256]{1,0:T(8,128)S(1)}, f32[128,256]{1,0:T(8,128)S(1)}, u32[]{:S(2)}, u32[]{:S(2)}) %collective-permute-start.5) | collective-permute-done | bytes 131104 | tf_op jit(solution)/shard_map/ppermute | solution.py:257
  25.2 3.9 %collective-permute-start.19 = (f32[128,256]{1,0:T(8,128)S(1)}, f32[128,256]{1,0:T(8,128)S(1)}, u32[]{:S(2)}, u32[]{:S(2)}) collective-permute-start(f32[128,256]{1,0:T(8,128)S(1)} %get-tuple-element.29), channel_id=1, source_target_pairs={{0,96},{32,0},{64,32},{96,64},{128,224},{160,128},{192,160},{224,1... | collective-permute-start | bytes 393224 | tf_op jit(solution)/shard_map/ppermute | solution.py:257
  29.1 6.5 %collective-permute-done.17.refs_0_.refs_3_ = f32[128,256]{1,0:T(8,128)S(1)} collective-permute-done((f32[128,256]{1,0:T(8,128)S(1)}, f32[128,256]{1,0:T(8,128)S(1)}, u32[]{:S(2)}, u32[]{:S(2)}) %collective-permute-start.17) | collective-permute-done | bytes 131104 | tf_op jit(solution)/shard_map/ppermute | solution.py:257
  37.6 8.7 %collective-permute-start.10 = (f32[256,512]{1,0:T(8,128)S(1)}, f32[256,512]{1,0:T(8,128)S(1)}, u32[]{:S(2)}, u32[]{:S(2)}) collective-permute-start(f32[256,512]{1,0:T(8,128)S(1)} %get-tuple-element.17._.mixed), channel_id=1, source_target_pairs={{8,6},{16,14},{24,22},{0,30},{30,0},{6,8},{14,16},{22,24},{9,7},{1... | collective-permute-start | bytes 1572872 | tf_op jit(solution)/shard_map/ppermute | solution.py:257
  47.0 2.1 %collective-permute-start.2 = (f32[384,256]{1,0:T(8,128)S(1)}, f32[384,256]{1,0:T(8,128)S(1)}, u32[]{:S(2)}, u32[]{:S(2)}) collective-permute-start(f32[384,256]{1,0:T(8,128)S(1)} %get-tuple-element.20), channel_id=1, source_target_pairs={{0,96},{32,0},{64,32},{96,64},{128,224},{160,128},{192,160},{224,1... | collective-permute-start | bytes 1179656 | tf_op jit(solution)/shard_map/ppermute | solution.py:257
  49.2 2.6 %collective-permute-start.20 = (f32[3,128,256]{2,1,0:T(8,128)S(1)}, f32[3,128,256]{2,1,0:T(8,128)S(1)}, u32[]{:S(2)}, u32[]{:S(2)}) collective-permute-start(f32[3,128,256]{2,1,0:T(8,128)S(1)} %shard_map.116.refs_3_), channel_id=1, source_target_pairs={{0,1},{1,0},{2,3},{3,2},{4,5},{5,4},{6,7},{7,6},{8,9},{9,8},{10,11... | collective-permute-start | bytes 1179656 | tf_op jit(solution)/shard_map/ppermute | solution.py:257
  51.9 4.8 %collective-permute-done.1.refs_1_ = f32[384,256]{1,0:T(8,128)S(1)} collective-permute-done((f32[384,256]{1,0:T(8,128)S(1)}, f32[384,256]{1,0:T(8,128)S(1)}, u32[]{:S(2)}, u32[]{:S(2)}) %collective-permute-start.1) | collective-permute-done | bytes 393248 | tf_op jit(solution)/shard_map/ppermute | solution.py:257
  56.8 4.9 %collective-permute-start.11 = (f32[256,512]{1,0:T(8,128)S(1)}, f32[256,512]{1,0:T(8,128)S(1)}, u32[]{:S(2)}, u32[]{:S(2)}) collective-permute-start(f32[256,512]{1,0:T(8,128)S(1)} %get-tuple-element.17._.mixed), channel_id=1, source_target_pairs={{16,0},{18,2},{20,4},{22,6},{24,8},{26,10},{28,12},{30,14},{0,16},... | collective-permute-start | bytes 1572872 | tf_op jit(solution)/shard_map/ppermute | solution.py:257
  61.6 4.6 %collective-permute-done.2.refs_2_ = f32[384,256]{1,0:T(8,128)S(1)} collective-permute-done((f32[384,256]{1,0:T(8,128)S(1)}, f32[384,256]{1,0:T(8,128)S(1)}, u32[]{:S(2)}, u32[]{:S(2)}) %collective-permute-start.2) | collective-permute-done | bytes 393248 | tf_op jit(solution)/shard_map/ppermute | solution.py:257
  67.5 4.0 %collective-permute-start.9 = (f32[256,512]{1,0:T(8,128)S(1)}, f32[256,512]{1,0:T(8,128)S(1)}, u32[]{:S(2)}, u32[]{:S(2)}) collective-permute-start(f32[256,512]{1,0:T(8,128)S(1)} %get-tuple-element.17._.mixed), channel_id=1, source_target_pairs={{0,2},{2,4},{4,6},{8,10},{10,12},{12,14},{16,18},{18,20},{20,22},{... | collective-permute-start | bytes 1572872 | tf_op jit(solution)/shard_map/ppermute | solution.py:257
  71.6 2.6 %collective-permute-start.6 = (f32[3,128,256]{2,1,0:T(8,128)S(1)}, f32[3,128,256]{2,1,0:T(8,128)S(1)}, u32[]{:S(2)}, u32[]{:S(2)}) collective-permute-start(f32[3,128,256]{2,1,0:T(8,128)S(1)} %shard_map.106.refs_3_), channel_id=1, source_target_pairs={{0,1},{1,0},{2,3},{3,2},{4,5},{5,4},{6,7},{7,6},{8,9},{9,8},{10,11... | collective-permute-start | bytes 1179656 | tf_op jit(solution)/shard_map/ppermute | solution.py:257
  83.9 4.2 %collective-permute-start.21 = (f32[256,256]{1,0:T(8,128)}, f32[256,256]{1,0:T(8,128)}, u32[]{:S(2)}, u32[]{:S(2)}) collective-permute-start(f32[256,256]{1,0:T(8,128)} %shard_map.118.refs_8_), channel_id=1, source_target_pairs={{0,128},{32,160},{64,192},{96,224},{128,0},{160,32},{192,64},{224,... | collective-permute-start | bytes 786440 | tf_op jit(solution)/shard_map/ppermute | solution.py:257
  91.8 4.2 %collective-permute-start.23 = (f32[264,256]{1,0:T(8,128)}, f32[264,256]{1,0:T(8,128)}, u32[]{:S(2)}, u32[]{:S(2)}) collective-permute-start(f32[264,256]{1,0:T(8,128)} %shard_map.110.refs_8_), channel_id=1, source_target_pairs={{0,128},{32,160},{64,192},{96,224},{128,0},{160,32},{192,64},{224,... | collective-permute-start | bytes 811016 | tf_op jit(solution)/shard_map/ppermute | solution.py:257
  100.3 18.3 %collective-permute-done.21.refs_11_ = f32[256,256]{1,0:T(8,128)} collective-permute-done((f32[256,256]{1,0:T(8,128)}, f32[256,256]{1,0:T(8,128)}, u32[]{:S(2)}, u32[]{:S(2)}) %collective-permute-start.21) | collective-permute-done | bytes 262176 | tf_op jit(solution)/shard_map/ppermute | solution.py:257
  118.6 5.6 %collective-permute-done.16.refs_10_ = f32[256,256]{1,0:T(8,128)} collective-permute-done((f32[256,256]{1,0:T(8,128)}, f32[256,256]{1,0:T(8,128)}, u32[]{:S(2)}, u32[]{:S(2)}) %collective-permute-start.16) | collective-permute-done | bytes 262176 | tf_op jit(solution)/shard_map/ppermute | solution.py:257
  128.0 3.9 %shard_map.119 = (f32[256,512]{1,0:T(8,128)}, f32[4,256]{1,0:T(4,128)S(1)}) custom-call(f32[8,256,256]{2,1,0:T(8,128)} %left.17, f32[8,512,256]{2,1,0:T(8,128)} %right.17, f32[384,256]{1,0:T(8,128)S(1)} %collective-permute-done.refs_0_, f32[384,256]{1,0:T(8,128)S(1)} %collective-permute-done.1.refs_1_, f32[384,256]{1,0:T(8,128)S(1)} %collective-permute-done.2.refs_2_, ...), custom_call_target="tpu_custom_call" | custom-call | flops 402653184 | bytes 1572864 | tf_op jit(solution)/shard_map/pallas_call | solution.py:284
  131.9 3.1 %shard_map.120.refs_9_ = f32[4,256]{1,0:T(4,128)S(1)} custom-call(f32[8,256,256]{2,1,0:T(8,128)} %left.17, f32[8,512,256]{2,1,0:T(8,128)} %right.17, f32[384,256]{1,0:T(8,128)S(1)} %collective-permute-done.12.refs_0_, f32[384,256]{1,0:T(8,128)S(1)} %collective-permute-done.13.refs_1_, f32[384,256]{1,0:T(8,128)S(1)} %collective-permute-done.14.refs_2_, ...), custom_call_target="tpu_custom_call" | custom-call | flops 402653184 | bytes 1572864 | tf_op jit(solution)/shard_map/pallas_call | solution.py:284
  135.9 3.0 %shard_map.121 = f32[4,256]{1,0:T(4,128)S(1)} custom-call(f32[8,256,256]{2,1,0:T(8,128)} %left.17, f32[8,512,256]{2,1,0:T(8,128)} %right.17, f32[384,256]{1,0:T(8,128)S(1)} %collective-permute-done.12.refs_0_, f32[384,256]{1,0:T(8,128)S(1)} %collective-permute-done.13.refs_1_, f32[384,256]{1,0:T(8,128)S(1)} %collective-permute-done.14.refs_2_, ...), custom_call_target="tpu_custom_call" | custom-call | flops 402653184 | bytes 1572864 | tf_op jit(solution)/shard_map/pallas_call | solution.py:284
  140.9 3.4 %collective-permute-start.26 = (f32[2,256]{1,0:T(2,128)S(1)}, f32[2,256]{1,0:T(2,128)S(1)}, u32[]{:S(2)}, u32[]{:S(2)}) collective-permute-start(f32[2,256]{1,0:T(2,128)S(1)} %bitcast.32), channel_id=1, source_target_pairs={{0,64},{32,96},{64,0},{96,32},{128,192},{160,224},{192,128},{224,1... | collective-permute-start | bytes 6152 | tf_op jit(solution)/shard_map/ppermute | solution.py:376
  (100 shorter events, 33.7 us)
Async XLA Ops:
  4.8 7.2 %collective-permute-start.3 = (f32[128,256]{1,0:T(8,128)S(1)}, f32[128,256]{1,0:T(8,128)S(1)}, u32[]{:S(2)}, u32[]{:S(2)}) collective-permute-start(f32[128,256]{1,0:T(8,128)S(1)} %get-tuple-element.21), channel_id=1, source_target_pairs={{0,32},{32,64},{64,96},{96,0},{128,160},{160,192},{192,224},{224,1... | collective-permute-start | bytes 393224 | tf_op jit(solution)/shard_map/ppermute | solution.py:257
  6.9 8.2 %collective-permute-start.4 = (f32[128,256]{1,0:T(8,128)S(1)}, f32[128,256]{1,0:T(8,128)S(1)}, u32[]{:S(2)}, u32[]{:S(2)}) collective-permute-start(f32[128,256]{1,0:T(8,128)S(1)} %get-tuple-element.22), channel_id=1, source_target_pairs={{0,64},{32,96},{64,0},{96,32},{128,192},{160,224},{192,128},{224,1... | collective-permute-start | bytes 393224 | tf_op jit(solution)/shard_map/ppermute | solution.py:257
  9.3 37.0 %collective-permute-start.12 = (f32[384,256]{1,0:T(8,128)S(1)}, f32[384,256]{1,0:T(8,128)S(1)}, u32[]{:S(2)}, u32[]{:S(2)}) collective-permute-start(f32[384,256]{1,0:T(8,128)S(1)} %get-tuple-element.24), channel_id=1, source_target_pairs={{0,32},{32,64},{64,96},{96,0},{128,160},{160,192},{192,224},{224,1... | collective-permute-start | bytes 1179656 | tf_op jit(solution)/shard_map/ppermute | solution.py:257
  9.3 37.7 %collective-permute-start.13 = (f32[384,256]{1,0:T(8,128)S(1)}, f32[384,256]{1,0:T(8,128)S(1)}, u32[]{:S(2)}, u32[]{:S(2)}) collective-permute-start(f32[384,256]{1,0:T(8,128)S(1)} %get-tuple-element.25), channel_id=1, source_target_pairs={{0,64},{32,96},{64,0},{96,32},{128,192},{160,224},{192,128},{224,1... | collective-permute-start | bytes 1179656 | tf_op jit(solution)/shard_map/ppermute | solution.py:257
  11.7 13.6 %collective-permute-start.5 = (f32[128,256]{1,0:T(8,128)S(1)}, f32[128,256]{1,0:T(8,128)S(1)}, u32[]{:S(2)}, u32[]{:S(2)}) collective-permute-start(f32[128,256]{1,0:T(8,128)S(1)} %get-tuple-element.23), channel_id=1, source_target_pairs={{0,96},{32,0},{64,32},{96,64},{128,224},{160,128},{192,160},{224,1... | collective-permute-start | bytes 393224 | tf_op jit(solution)/shard_map/ppermute | solution.py:257
  12.0 23.6 %collective-permute-start.17 = (f32[128,256]{1,0:T(8,128)S(1)}, f32[128,256]{1,0:T(8,128)S(1)}, u32[]{:S(2)}, u32[]{:S(2)}) collective-permute-start(f32[128,256]{1,0:T(8,128)S(1)} %get-tuple-element.27), channel_id=1, source_target_pairs={{0,32},{32,64},{64,96},{96,0},{128,160},{160,192},{192,224},{224,1... | collective-permute-start | bytes 393224 | tf_op jit(solution)/shard_map/ppermute | solution.py:257
  15.0 22.5 %collective-permute-start.18 = (f32[128,256]{1,0:T(8,128)S(1)}, f32[128,256]{1,0:T(8,128)S(1)}, u32[]{:S(2)}, u32[]{:S(2)}) collective-permute-start(f32[128,256]{1,0:T(8,128)S(1)} %get-tuple-element.28), channel_id=1, source_target_pairs={{0,64},{32,96},{64,0},{96,32},{128,192},{160,224},{192,128},{224,1... | collective-permute-start | bytes 393224 | tf_op jit(solution)/shard_map/ppermute | solution.py:257
  25.2 12.3 %collective-permute-start.19 = (f32[128,256]{1,0:T(8,128)S(1)}, f32[128,256]{1,0:T(8,128)S(1)}, u32[]{:S(2)}, u32[]{:S(2)}) collective-permute-start(f32[128,256]{1,0:T(8,128)S(1)} %get-tuple-element.29), channel_id=1, source_target_pairs={{0,96},{32,0},{64,32},{96,64},{128,224},{160,128},{192,160},{224,1... | collective-permute-start | bytes 393224 | tf_op jit(solution)/shard_map/ppermute | solution.py:257
  35.7 13.5 %collective-permute-start.14 = (f32[384,256]{1,0:T(8,128)S(1)}, f32[384,256]{1,0:T(8,128)S(1)}, u32[]{:S(2)}, u32[]{:S(2)}) collective-permute-start(f32[384,256]{1,0:T(8,128)S(1)} %get-tuple-element.26), channel_id=1, source_target_pairs={{0,96},{32,0},{64,32},{96,64},{128,224},{160,128},{192,160},{224,1... | collective-permute-start | bytes 1179656 | tf_op jit(solution)/shard_map/ppermute | solution.py:257
  37.6 14.3 %collective-permute-start = (f32[384,256]{1,0:T(8,128)S(1)}, f32[384,256]{1,0:T(8,128)S(1)}, u32[]{:S(2)}, u32[]{:S(2)}) collective-permute-start(f32[384,256]{1,0:T(8,128)S(1)} %get-tuple-element.18), channel_id=1, source_target_pairs={{0,32},{32,64},{64,96},{96,0},{128,160},{160,192},{192,224},{224,1... | collective-permute-start | bytes 1179656 | tf_op jit(solution)/shard_map/ppermute | solution.py:257
  37.6 29.9 %collective-permute-start.10 = (f32[256,512]{1,0:T(8,128)S(1)}, f32[256,512]{1,0:T(8,128)S(1)}, u32[]{:S(2)}, u32[]{:S(2)}) collective-permute-start(f32[256,512]{1,0:T(8,128)S(1)} %get-tuple-element.17._.mixed), channel_id=1, source_target_pairs={{8,6},{16,14},{24,22},{0,30},{30,0},{6,8},{14,16},{22,24},{9,7},{1... | collective-permute-start | bytes 1572872 | tf_op jit(solution)/shard_map/ppermute | solution.py:257
  46.3 10.5 %collective-permute-start.1 = (f32[384,256]{1,0:T(8,128)S(1)}, f32[384,256]{1,0:T(8,128)S(1)}, u32[]{:S(2)}, u32[]{:S(2)}) collective-permute-start(f32[384,256]{1,0:T(8,128)S(1)} %get-tuple-element.19), channel_id=1, source_target_pairs={{0,64},{32,96},{64,0},{96,32},{128,192},{160,224},{192,128},{224,1... | collective-permute-start | bytes 1179656 | tf_op jit(solution)/shard_map/ppermute | solution.py:257
  47.0 19.2 %collective-permute-start.2 = (f32[384,256]{1,0:T(8,128)S(1)}, f32[384,256]{1,0:T(8,128)S(1)}, u32[]{:S(2)}, u32[]{:S(2)}) collective-permute-start(f32[384,256]{1,0:T(8,128)S(1)} %get-tuple-element.20), channel_id=1, source_target_pairs={{0,96},{32,0},{64,32},{96,64},{128,224},{160,128},{192,160},{224,1... | collective-permute-start | bytes 1179656 | tf_op jit(solution)/shard_map/ppermute | solution.py:257
  49.2 22.4 %collective-permute-start.20 = (f32[3,128,256]{2,1,0:T(8,128)S(1)}, f32[3,128,256]{2,1,0:T(8,128)S(1)}, u32[]{:S(2)}, u32[]{:S(2)}) collective-permute-start(f32[3,128,256]{2,1,0:T(8,128)S(1)} %shard_map.116.refs_3_), channel_id=1, source_target_pairs={{0,1},{1,0},{2,3},{3,2},{4,5},{5,4},{6,7},{7,6},{8,9},{9,8},{10,11... | collective-permute-start | bytes 1179656 | tf_op jit(solution)/shard_map/ppermute | solution.py:257
  51.8 22.4 %collective-permute-start.15 = (f32[3,128,256]{2,1,0:T(8,128)S(1)}, f32[3,128,256]{2,1,0:T(8,128)S(1)}, u32[]{:S(2)}, u32[]{:S(2)}) collective-permute-start(f32[3,128,256]{2,1,0:T(8,128)S(1)} %shard_map.113.refs_3_), channel_id=1, source_target_pairs={{0,1},{1,0},{2,3},{3,2},{4,5},{5,4},{6,7},{7,6},{8,9},{9,8},{10,11... | collective-permute-start | bytes 1179656 | tf_op jit(solution)/shard_map/ppermute | solution.py:257
  56.8 27.2 %collective-permute-start.11 = (f32[256,512]{1,0:T(8,128)S(1)}, f32[256,512]{1,0:T(8,128)S(1)}, u32[]{:S(2)}, u32[]{:S(2)}) collective-permute-start(f32[256,512]{1,0:T(8,128)S(1)} %get-tuple-element.17._.mixed), channel_id=1, source_target_pairs={{16,0},{18,2},{20,4},{22,6},{24,8},{26,10},{28,12},{30,14},{0,16},... | collective-permute-start | bytes 1572872 | tf_op jit(solution)/shard_map/ppermute | solution.py:257
  66.2 21.9 %collective-permute-start.8 = (f32[256,512]{1,0:T(8,128)S(1)}, f32[256,512]{1,0:T(8,128)S(1)}, u32[]{:S(2)}, u32[]{:S(2)}) collective-permute-start(f32[256,512]{1,0:T(8,128)S(1)} %get-tuple-element.17._.mixed), channel_id=1, source_target_pairs={{2,0},{4,2},{6,4},{10,8},{12,10},{14,12},{18,16},{20,18},{22,20},{... | collective-permute-start | bytes 1572872 | tf_op jit(solution)/shard_map/ppermute | solution.py:257
  67.5 21.8 %collective-permute-start.9 = (f32[256,512]{1,0:T(8,128)S(1)}, f32[256,512]{1,0:T(8,128)S(1)}, u32[]{:S(2)}, u32[]{:S(2)}) collective-permute-start(f32[256,512]{1,0:T(8,128)S(1)} %get-tuple-element.17._.mixed), channel_id=1, source_target_pairs={{0,2},{2,4},{4,6},{8,10},{10,12},{12,14},{16,18},{18,20},{20,22},{... | collective-permute-start | bytes 1572872 | tf_op jit(solution)/shard_map/ppermute | solution.py:257
  71.6 19.0 %collective-permute-start.6 = (f32[3,128,256]{2,1,0:T(8,128)S(1)}, f32[3,128,256]{2,1,0:T(8,128)S(1)}, u32[]{:S(2)}, u32[]{:S(2)}) collective-permute-start(f32[3,128,256]{2,1,0:T(8,128)S(1)} %shard_map.106.refs_3_), channel_id=1, source_target_pairs={{0,1},{1,0},{2,3},{3,2},{4,5},{5,4},{6,7},{7,6},{8,9},{9,8},{10,11... | collective-permute-start | bytes 1179656 | tf_op jit(solution)/shard_map/ppermute | solution.py:257
  74.2 23.7 %collective-permute-start.7 = (f32[3,128,256]{2,1,0:T(8,128)S(1)}, f32[3,128,256]{2,1,0:T(8,128)S(1)}, u32[]{:S(2)}, u32[]{:S(2)}) collective-permute-start(f32[3,128,256]{2,1,0:T(8,128)S(1)} %shard_map.107.refs_3_), channel_id=1, source_target_pairs={{0,1},{1,0},{2,3},{3,2},{4,5},{5,4},{6,7},{7,6},{8,9},{9,8},{10,11... | collective-permute-start | bytes 1179656 | tf_op jit(solution)/shard_map/ppermute | solution.py:257
  83.9 34.7 %collective-permute-start.21 = (f32[256,256]{1,0:T(8,128)}, f32[256,256]{1,0:T(8,128)}, u32[]{:S(2)}, u32[]{:S(2)}) collective-permute-start(f32[256,256]{1,0:T(8,128)} %shard_map.118.refs_8_), channel_id=1, source_target_pairs={{0,128},{32,160},{64,192},{96,224},{128,0},{160,32},{192,64},{224,... | collective-permute-start | bytes 786440 | tf_op jit(solution)/shard_map/ppermute | solution.py:257
  88.1 36.1 %collective-permute-start.16 = (f32[256,256]{1,0:T(8,128)}, f32[256,256]{1,0:T(8,128)}, u32[]{:S(2)}, u32[]{:S(2)}) collective-permute-start(f32[256,256]{1,0:T(8,128)} %shard_map.115.refs_5_), channel_id=1, source_target_pairs={{0,128},{32,160},{64,192},{96,224},{128,0},{160,32},{192,64},{224,... | collective-permute-start | bytes 786440 | tf_op jit(solution)/shard_map/ppermute | solution.py:257
  91.8 40.1 %collective-permute-start.23 = (f32[264,256]{1,0:T(8,128)}, f32[264,256]{1,0:T(8,128)}, u32[]{:S(2)}, u32[]{:S(2)}) collective-permute-start(f32[264,256]{1,0:T(8,128)} %shard_map.110.refs_8_), channel_id=1, source_target_pairs={{0,128},{32,160},{64,192},{96,224},{128,0},{160,32},{192,64},{224,... | collective-permute-start | bytes 811016 | tf_op jit(solution)/shard_map/ppermute | solution.py:257
  99.1 36.7 %collective-permute-start.22 = (f32[264,256]{1,0:T(8,128)}, f32[264,256]{1,0:T(8,128)}, u32[]{:S(2)}, u32[]{:S(2)}) collective-permute-start(f32[264,256]{1,0:T(8,128)} %shard_map.112.refs_9_), channel_id=1, source_target_pairs={{0,128},{32,160},{64,192},{96,224},{128,0},{160,32},{192,64},{224,... | collective-permute-start | bytes 811016 | tf_op jit(solution)/shard_map/ppermute | solution.py:257
  (23 other events, 315.6 us)
where the time goes:
time: 148 us; the launch traced here: 147 us
  waiting for transfers between devices  57.3 us (39%)
  starting transfers between devices  55.5 us (38%)
  Pallas kernels  27.7 us (19%)
  local copies, waits for them, and re-layouts  4.41 us (3%)
  between operations  2.37 us (2%)
    ppermute x24, waiting for transfers between devices, send(): return lax.ppermute(value, axis, pairs)  54.1 us
    ppermute x24, starting transfers between devices, send(): return lax.ppermute(value, axis, pairs)  51 us
    pallas_call x7, Pallas kernels, work(): pl.pallas_call(functools.partial(kernel, ring, own, which), in_specs=[ANY...  17.5 us
    unnamed x42, local copies, waits for them, and re-layouts  3.79 us
    ppermute x3, starting transfers between devices, body(): lax.ppermute(both[by], 'fit', shifted(-by))  3.44 us
  transfers between devices with their start and end apart: 28, of which 13 were waited for; matrix products, arithmetic and copies ran while one was open for 0% of the time, Pallas kernels for 14%

commit v1 on v0

--- a/solution.py
+++ b/solution.py
@@ -58,8 +58,22 @@
     return copies
 
 
-def pack_kernel(ring, own, left, right, _, *refs):
-    for copy in fill_packs(ring, own, left, right, refs[:-1], refs[-1]):
+def pack_kernel(ring, own, occ, dom, left, right, vir, _, *refs):
+    *packs, facts, sems = refs
+    copies = fill_packs(ring, own, left, right, packs, sems)
+    rows, width = left.shape[1], vir.shape[1]
+    part = width // 4
+    core = lax.axis_index("blk")
+    for which in range(facts.shape[0]):
+        facts[which] = jnp.concatenate([
+            jnp.concatenate([vir[:, spot] for spot in columns(part, which)], axis=1),
+            vir[:, pl.ds(pl.multiple_of(core * rows, rows), rows)],
+            jnp.full((1, 2 * part), occ[0], F32),
+            jnp.full((1, 2 * part), (dom[0] * part).astype(F32), F32),
+            jnp.concatenate([vir[:, spot] for spot in columns(part, 1)], axis=1),
+            jnp.zeros((EXTRA - 5, 2 * part), F32),
+        ])
+    for copy in copies:
         copy.wait()
 
 
@@ -132,26 +146,27 @@
     out_ref[...] = finished(part_ref, packs, others)
 
 
-def denominators(facts, rows):
+def denominators(facts, rows, at=0):
     width = facts.shape[1]
     column = jnp.broadcast_to(facts[1:2, 0:rows], (128, rows)).T
-    return jnp.concatenate([column] * (width // 128), axis=1) + facts[0:1, :] + facts[2:3, 0:1]
-
-
-def residual_kernel(which, occ, dom, part_ref, *refs):
-    *packs, others, amp, corr, vir, out_ref = refs
-    rows, width = amp.shape
-    part = others.shape[1]
-    spots = columns(part, which)
+    return jnp.concatenate([column] * (width // 128), axis=1) + facts[at : at + 1, :] + facts[2:3, 0:1]
+
+
+def inside(facts, rows, part, which):
     core = lax.axis_index("blk")
-    out_ref[rows:, :] = jnp.concatenate([
-        jnp.concatenate([vir[:, spot] for spot in spots], axis=1),
-        vir[:, pl.ds(pl.multiple_of(core * rows, rows), rows)],
-        jnp.full((1, 2 * part), occ[0], F32),
-        jnp.full((1, 2 * part), (dom[0] * (width // 4)).astype(F32), F32),
-        jnp.zeros((EXTRA - 4, 2 * part), F32),
-    ])
-    below = denominators(out_ref.at[rows : rows + EXTRA], rows)
+    row = (core * rows + lax.broadcasted_iota(jnp.int32, (rows, 2 * part), 0)).astype(F32)
+    lane = lax.broadcasted_iota(jnp.int32, (rows, 2 * part), 1)
+    offset = jnp.where(lane < part, 2 * core * part, (1 - 2 * core) * part) + which * part
+    limit = facts[3:4, 0:1]
+    return (row < limit) & ((lane + offset).astype(F32) < limit)
+
+
+def residual_kernel(which, part_ref, *refs):
+    *packs, others, amp, corr, facts, out_ref = refs
+    rows = amp.shape[0]
+    spots = columns(others.shape[1], which)
+    out_ref[rows:, :] = facts[which]
+    below = denominators(facts.at[which], rows)
     old = jnp.concatenate([amp[:, spot] for spot in spots], axis=1)
     fixed = below * old - jnp.concatenate([corr[:, spot] for spot in spots], axis=1)
     residual = finished(part_ref, packs, others) + fixed
@@ -165,28 +180,31 @@
     shorts = take(ring - 1) if 1 in which else []
     others = dict(zip(which, take(len(which))))
     early, late = take(len(which)), take(len(which))
-    before = None if 0 in which else take(1)[0]
-    new_ref = take(1)[0] if own else None
-    sums_ref, left_here, right_here, sems = refs
+    new_ref = take(1)[0]
+    sums_ref, left_here, right_here, sems, *staged = refs
+    if staged:
+        *held, more_sems = staged
+        sources = longs + shorts + list(others.values())
+        arrivals = [pltpu.make_async_copy(a, b, more_sems.at[i]) for i, (a, b) in enumerate(zip(sources, held))]
+        for copy in arrivals:
+            copy.start()
+        longs, shorts = held[: len(longs)], held[len(longs) : len(longs) + len(shorts)]
+        others = dict(zip(which, held[len(longs) + len(shorts) :]))
     copies = fetch(ring, own, left, right, left_here, right_here, sems)
     rows, part = late[0].shape[0], late[0].shape[1] // 2
-    core = lax.axis_index("blk")
-    row = (core * rows + lax.broadcasted_iota(jnp.int32, (rows, 2 * part), 0)).astype(F32)
-    lane = lax.broadcasted_iota(jnp.int32, (rows, 2 * part), 1)
     new = {}
     for w, block, term in zip(which, early, late):
         facts = block.at[rows : rows + EXTRA]
-        below = denominators(facts, rows)
-        offset = jnp.where(lane < part, 2 * core * part, (1 - 2 * core) * part) + w * part
-        column = (lane + offset).astype(F32)
-        limit = facts[3:4, 0:1]
-        updated = block[0:rows, :] - 0.7 * term[...] / below
-        value = jnp.where((row < limit) & (column < limit), updated, 0.0)
-        if own:
-            mine, yours = columns(part, w)
-            new_ref[:, mine] = value[:, 0:part]
-            new_ref[:, yours] = value[:, part:]
+        updated = block[0:rows, :] - 0.7 * term[...] / denominators(facts, rows)
+        value = jnp.where(inside(facts, rows, part, w), updated, 0.0)
+        mine, yours = columns(part, w)
+        new_ref[:, mine] = value[:, 0:part]
+        new_ref[:, yours] = value[:, part:]
         new[w] = halves(value)
+
+    if staged:
+        for copy in arrivals:
+            copy.wait()
 
     def add_up(spot, lefts, rights):
         product = None
@@ -204,8 +222,43 @@
     for copy in copies:
         copy.wait()
     add_up(0, left_here[...], lambda w: jnp.concatenate([right_here[spot, :] for spot in columns(part, w)], axis=0))
-    if before is not None:
-        sums_ref[...] += before[...]
+
+
+def density_first_kernel(ring, own, left, right, *refs):
+    *packs, block, term, later_term, sums_ref, top_ref, low_ref, own_left, base_ref, keep_ref, right_here, sems = refs
+    longs, shorts, (others, later_others) = packs[: ring - 1], packs[ring - 1 : 2 * ring - 2], packs[2 * ring - 2 :]
+    copies = fetch(ring, own, left, right, own_left, right_here, sems)
+    rows, part = term.shape[0], term.shape[1] // 2
+    facts = block.at[rows : rows + EXTRA]
+    updated = block[0:rows, :] - 0.7 * term[...] / denominators(facts, rows)
+    value = halves(jnp.where(inside(facts, rows, part, 0), updated, 0.0))
+    base_ref[...] = 0.7 * later_term[...] / denominators(facts, rows, 4)
+    keep_ref[...] = jnp.where(inside(facts, rows, part, 1), 1.0, 0.0)
+
+    def prepare(spot, mine, yours):
+        for i, source in enumerate((mine, yours)):
+            top_ref[spot, i * part : (i + 1) * part, :], low_ref[spot, i * part : (i + 1) * part, :] = halves(source)
+
+    def add_up(spot, lefts, mine, yours):
+        product = dot3(value, halves(jnp.concatenate([mine, yours], axis=0)), NN)
+        sums_ref[spot : spot + 1, :] = jnp.sum(lefts * product, axis=0, keepdims=True)
+
+    for i, (long, short) in enumerate(zip(longs, shorts)):
+        add_up(i + 1, long[0:rows, :], long[rows:, :], others[i])
+        prepare(i + 1, short[...], later_others[i])
+    for copy in copies:
+        copy.wait()
+    add_up(0, own_left[...], *[right_here[spot, :] for spot in columns(part, 0)])
+    prepare(0, *[right_here[spot, :] for spot in columns(part, 1)])
+
+
+def density_last_kernel(block, base, keep, top, low, own_left, *refs):
+    *longs, before, sums_ref = refs
+    rows = base.shape[0]
+    value = halves(jnp.where(keep[...] > 0.0, block[0:rows, :] - base[...], 0.0))
+    for spot, long in enumerate((own_left, *longs)):
+        product = dot3(value, (top[spot], low[spot]), NN)
+        sums_ref[spot : spot + 1, :] = before[spot : spot + 1, :] + jnp.sum(long[0:rows, :] * product, axis=0, keepdims=True)
 
 
 def correction_kernel(pairs_per_shard, shards, neighbours, coupling, mixed, up, down, wrap, far, d_ref, out_ref):
@@ -280,20 +333,22 @@
         )(*vmem(*values))
         return gathered, send(gathered, "blk", swap)
 
-    def work(kernel, own, which, factors, extras, outs):
+    def work(kernel, own, which, factors, extras, outs, resident=True):
+        held = [pltpu.VMEM(a.shape, F32) for a in factors] + [pltpu.SemaphoreType.DMA((len(factors),))]
         return pl.pallas_call(
             functools.partial(kernel, ring, own, which),
-            in_specs=[ANY] * 2 + [WHOLE] * (len(factors) + len(extras)),
+            in_specs=[ANY] * 2 + [WHOLE if resident else ANY] * len(factors) + [WHOLE] * len(extras),
             out_specs=[WHOLE] * len(outs),
             out_shape=outs,
             scratch_shapes=[
                 pltpu.VMEM((rows, depth), F32),
                 pltpu.VMEM((width, depth), F32),
                 pltpu.SemaphoreType.DMA((2,)),
+                *([] if resident else held),
             ],
             compiler_params=LIMIT,
             cost_estimate=cost(3 * rows * width * depth * ring, 2 * ring * depth * (rows + width)),
-        )(*hbm(left, right), *vmem(*factors, *extras))
+        )(*hbm(left, right), *(vmem if resident else hbm)(*factors), *vmem(*extras))
 
     *sent, mixed = pl.pallas_call(
         functools.partial(head_kernel, ring),
@@ -312,15 +367,15 @@
         from_shards(mixed, [(s, s + 1) for s in shards if s % SEGMENT == SEGMENT - 1] + [(s, s - 1) for s in shards if s % SEGMENT == 0]),
         from_shards(mixed, [(s, s + pair_count // 2) for s in shards]),
     ]
-    sent = pl.pallas_call(
+    *sent, facts = pl.pallas_call(
         functools.partial(pack_kernel, ring, True),
-        in_specs=[ANY] * 3,
-        out_specs=[WHOLE] * len(packs),
-        out_shape=packs,
+        in_specs=[SCALARS] * 2 + [ANY] * 2 + [WHOLE, ANY],
+        out_specs=[WHOLE] * (1 + len(packs)),
+        out_shape=packs + [jax.ShapeDtypeStruct((2, EXTRA, 2 * part), F32)],
         scratch_shapes=[pack_sems],
         compiler_params=LIMIT,
         cost_estimate=cost(0, 24 * rows * width),
-    )(*hbm(left, right), mixed)
+    )(occ_energy, dom_blocks, *hbm(left, right), vir_energy, mixed)
     my_longs, my_shorts = spread(sent[: ring - 1]), spread(sent[ring - 1 :])
     (corr,) = pl.pallas_call(
         functools.partial(correction_kernel, fit_count, pair_count),
@@ -352,25 +407,37 @@
         (started,) = work(integral_kernel, True, which, (*my_longs, gathered), (), [some])
         done = pl.pallas_call(
             functools.partial(residual_kernel, which),
-            in_specs=[SCALARS] * 2 + [WHOLE] * (5 + len(my_longs)),
+            in_specs=[WHOLE] * (5 + len(my_longs)),
             out_specs=WHOLE,
             out_shape=some_long,
             compiler_params=LIMIT,
             cost_estimate=cost(2 * rows * width * depth, 24 * rows * width),
-        )(occ_energy, dom_blocks, started, *vmem(*my_longs, other), amp, corr, vir_energy)
+        )(started, *vmem(*my_longs, other), amp, corr, facts)
         my_others.append(other)
         my_early.append(done)
         their_early.append(send(done, "fit", across))
     new, my_sums = work(
-        density_kernel, True, (0, 1), (*my_longs, *my_shorts, *my_others), (*my_early, *my_late), [block, sums]
+        density_kernel, True, (0, 1), (*my_longs, *my_shorts, *my_others), (*my_early, *my_late), [block, sums], resident=False
     )
-    (their_sums,) = work(
-        density_kernel, False, (0,), (*their_longs, their_others[0]), (their_early[0], their_parts[0]), [sums]
-    )
-    (their_sums,) = work(
-        density_kernel, False, (1,), (*their_longs, *their_shorts, their_others[1]),
-        (their_early[1], their_parts[1], their_sums), [sums],
-    )
+    square = jax.ShapeDtypeStruct((rows, depth), F32)
+    ready = jax.ShapeDtypeStruct((ring, 2 * part, depth), jnp.bfloat16)
+    their_sums, top, low, own_left, base, keep = pl.pallas_call(
+        functools.partial(density_first_kernel, ring, False),
+        in_specs=[ANY] * 2 + [WHOLE] * (2 * ring + 3),
+        out_specs=[WHOLE] * 6,
+        out_shape=[sums, ready, ready, square, some, some],
+        scratch_shapes=[pltpu.VMEM((width, depth), F32), pltpu.SemaphoreType.DMA((2,))],
+        compiler_params=LIMIT,
+        cost_estimate=cost(3 * rows * width * depth * ring, 2 * ring * depth * (rows + width)),
+    )(*hbm(left, right), *vmem(*their_longs, *their_shorts, *their_others, their_early[0], *their_parts))
+    their_sums = pl.pallas_call(
+        density_last_kernel,
+        in_specs=[WHOLE] * (ring + 6),
+        out_specs=WHOLE,
+        out_shape=sums,
+        compiler_params=LIMIT,
+        cost_estimate=cost(3 * rows * width * depth * ring, ring * depth * (rows + width)),
+    )(*vmem(their_early[1], base, keep, top, low, own_left, *their_longs, their_sums))
     both = jnp.stack([my_sums, their_sums], axis=1)
     both = both + lax.ppermute(both, "blk", swap)
     parts = [both[0]] + [lax.ppermute(both[by], "fit", shifted(-by)) for by in range(1, ring)]

time: 148 us -> 144 us (0.973)
  starting transfers between devices: 55.5 us -> 78.3 us
  waiting for transfers between devices: 57.3 us -> 36.1 us
  local copies, waits for them, and re-layouts: 4.41 us -> 0.72 us
  Pallas kernels: 27.7 us -> 25.5 us
    ppermute x24, waiting for transfers between devices: 54.1 us -> 33.1 us  [send(): return lax.ppermute(value, axis, pairs)]
    ppermute x3, starting transfers between devices: 3.44 us -> 22.1 us  [body(): lax.ppermute(both[by], 'fit', shifted(-by))]
    pallas_call x7 -> x5, Pallas kernels: 17.5 us -> 12.3 us  [work(): pl.pallas_call(functools.partial(kernel, ring, own, which), in_specs=[ANY...]
    ppermute x24, starting transfers between devices: 51 us -> 55.2 us  [send(): return lax.ppermute(value, axis, pairs)]
    unnamed x42 -> x46, local copies, waits for them, and re-layouts: 3.79 us -> 0.1 us
    pallas_call x3 -> x5, Pallas kernels: 3.92 us -> 6.9 us  [the longest x1 3.07 us: body(): pl.pallas_call(functools.partial(density_first_kernel, ring, False), in_s...]
  transfers between devices with their start and end apart: 28 -> 28, of which waited for: 13 -> 11; matrix products, arithmetic and copies ran while one was open for 0% -> 0% of each run, Pallas kernels for 14% -> 16%
where the time goes in v1:
time: 144 us; the launch traced here: 143 us
  starting transfers between devices  78.3 us (54%)
  waiting for transfers between devices  36.1 us (25%)
  Pallas kernels  25.5 us (18%)
  between operations  2.39 us (2%)
    ppermute x24, starting transfers between devices, send(): return lax.ppermute(value, axis, pairs)  55.2 us
    ppermute x24, waiting for transfers between devices, send(): return lax.ppermute(value, axis, pairs)  33.1 us
    ppermute x3, starting transfers between devices, body(): lax.ppermute(both[by], 'fit', shifted(-by))  22.1 us
    pallas_call x5, Pallas kernels, work(): pl.pallas_call(functools.partial(kernel, ring, own, which), in_specs=[ANY...  12.3 us
    pallas_call x1, Pallas kernels, body(): pl.pallas_call(functools.partial(density_first_kernel, ring, False), in_s...  3.07 us
  transfers between devices with their start and end apart: 28, of which 11 were waited for; matrix products, arithmetic and copies ran while one was open for 0% of the time, Pallas kernels for 16%

profile of v1, /device:TPU:1, one launch (start us, length us, event | category | flops | bytes accessed | tf_op | source)
XLA Modules:
  0.0 143.1 jit_solution(16647966070923371703)
XLA Ops:
  0.6 2.6 %shard_map.104 = (f32[384,256]{1,0:T(8,128)S(1)}, f32[384,256]{1,0:T(8,128)S(1)}, f32[384,256]{1,0:T(8,128)S(1)}, f32[128,256]{1,0:T(8,128)S(1)}, f32[128,256]{1...) custom-call(f32[8,256,256]{2,1,0:T(8,128)} %left.15, f32[8,512,256]{2,1,0:T(8,128)} %right.15, ...), custom_call_target="tpu_custom_call" | custom-call | flops 402653184 | bytes 4194304 | tf_op jit(solution)/shard_map/pallas_call | solution.py:353
  3.3 2.1 %collective-permute-start.17 = (f32[128,256]{1,0:T(8,128)S(1)}, f32[128,256]{1,0:T(8,128)S(1)}, u32[]{:S(2)}, u32[]{:S(2)}) collective-permute-start(f32[128,256]{1,0:T(8,128)S(1)} %get-tuple-element.35), channel_id=1, source_target_pairs={{0,32},{32,64},{64,96},{96,0},{128,160},{160,192},{192,224},{224,1... | collective-permute-start | bytes 393224 | tf_op jit(solution)/shard_map/ppermute | solution.py:310
  5.4 2.4 %collective-permute-start.18 = (f32[128,256]{1,0:T(8,128)S(1)}, f32[128,256]{1,0:T(8,128)S(1)}, u32[]{:S(2)}, u32[]{:S(2)}) collective-permute-start(f32[128,256]{1,0:T(8,128)S(1)} %get-tuple-element.36), channel_id=1, source_target_pairs={{0,64},{32,96},{64,0},{96,32},{128,192},{160,224},{192,128},{224,1... | collective-permute-start | bytes 393224 | tf_op jit(solution)/shard_map/ppermute | solution.py:310
  15.2 1.9 %collective-permute-start.4 = (f32[128,256]{1,0:T(8,128)S(1)}, f32[128,256]{1,0:T(8,128)S(1)}, u32[]{:S(2)}, u32[]{:S(2)}) collective-permute-start(f32[128,256]{1,0:T(8,128)S(1)} %get-tuple-element.29), channel_id=1, source_target_pairs={{0,64},{32,96},{64,0},{96,32},{128,192},{160,224},{192,128},{224,1... | collective-permute-start | bytes 393224 | tf_op jit(solution)/shard_map/ppermute | solution.py:310
  17.1 18.3 %collective-permute-done.3.refs_0_.refs_3_ = f32[128,256]{1,0:T(8,128)S(1)} collective-permute-done((f32[128,256]{1,0:T(8,128)S(1)}, f32[128,256]{1,0:T(8,128)S(1)}, u32[]{:S(2)}, u32[]{:S(2)}) %collective-permute-start.3) | collective-permute-done | bytes 131104 | tf_op jit(solution)/shard_map/ppermute | solution.py:310
  36.1 2.0 %collective-permute-start.5 = (f32[128,256]{1,0:T(8,128)S(1)}, f32[128,256]{1,0:T(8,128)S(1)}, u32[]{:S(2)}, u32[]{:S(2)}) collective-permute-start(f32[128,256]{1,0:T(8,128)S(1)} %get-tuple-element.30), channel_id=1, source_target_pairs={{0,96},{32,0},{64,32},{96,64},{128,224},{160,128},{192,160},{224,1... | collective-permute-start | bytes 393224 | tf_op jit(solution)/shard_map/ppermute | solution.py:310
  38.0 1.9 %collective-permute-done.5.refs_2_.refs_5_ = f32[128,256]{1,0:T(8,128)S(1)} collective-permute-done((f32[128,256]{1,0:T(8,128)S(1)}, f32[128,256]{1,0:T(8,128)S(1)}, u32[]{:S(2)}, u32[]{:S(2)}) %collective-permute-start.5) | collective-permute-done | bytes 131104 | tf_op jit(solution)/shard_map/ppermute | solution.py:310
  40.0 1.9 %collective-permute-start.1 = (f32[384,256]{1,0:T(8,128)S(1)}, f32[384,256]{1,0:T(8,128)S(1)}, u32[]{:S(2)}, u32[]{:S(2)}) collective-permute-start(f32[384,256]{1,0:T(8,128)S(1)} %get-tuple-element.26), channel_id=1, source_target_pairs={{0,64},{32,96},{64,0},{96,32},{128,192},{160,224},{192,128},{224,1... | collective-permute-start | bytes 1179656 | tf_op jit(solution)/shard_map/ppermute | solution.py:310
  43.1 3.9 %collective-permute-start.20 = (f32[3,128,256]{2,1,0:T(8,128)S(1)}, f32[3,128,256]{2,1,0:T(8,128)S(1)}, u32[]{:S(2)}, u32[]{:S(2)}) collective-permute-start(f32[3,128,256]{2,1,0:T(8,128)S(1)} %shard_map.116.refs_3_), channel_id=1, source_target_pairs={{0,1},{1,0},{2,3},{3,2},{4,5},{5,4},{6,7},{7,6},{8,9},{9,8},{10,11... | collective-permute-start | bytes 1179656 | tf_op jit(solution)/shard_map/ppermute | solution.py:310
  48.4 8.1 %collective-permute-start.15 = (f32[3,128,256]{2,1,0:T(8,128)S(1)}, f32[3,128,256]{2,1,0:T(8,128)S(1)}, u32[]{:S(2)}, u32[]{:S(2)}) collective-permute-start(f32[3,128,256]{2,1,0:T(8,128)S(1)} %shard_map.113.refs_3_), channel_id=1, source_target_pairs={{0,1},{1,0},{2,3},{3,2},{4,5},{5,4},{6,7},{7,6},{8,9},{9,8},{10,11... | collective-permute-start | bytes 1179656 | tf_op jit(solution)/shard_map/ppermute | solution.py:310
  56.5 7.3 %collective-permute-start.10 = (f32[256,512]{1,0:T(8,128)S(1)}, f32[256,512]{1,0:T(8,128)S(1)}, u32[]{:S(2)}, u32[]{:S(2)}) collective-permute-start(f32[256,512]{1,0:T(8,128)S(1)} %get-tuple-element.24._.mixed), channel_id=1, source_target_pairs={{8,6},{16,14},{24,22},{0,30},{30,0},{6,8},{14,16},{22,24},{9,7},{1... | collective-permute-start | bytes 1572872 | tf_op jit(solution)/shard_map/ppermute | solution.py:310
  67.4 1.9 %shard_map.117.part_ref = f32[256,256]{1,0:T(8,128)S(1)} custom-call(f32[8,256,256]{2,1,0:T(8,128)} %left.15, f32[8,512,256]{2,1,0:T(8,128)} %right.15, f32[384,256]{1,0:T(8,128)S(1)} %collective-permute-done.12.refs_0_, f32[384,256]{1,0:T(8,128)S(1)} %collective-permute-done.13.refs_1_, f32[384,256]{1,0:T(8,128)S(1)} %collective-permute-done.14.refs_2_, ...), custom_call_target="tpu_custom_call" | custom-call | flops 402653184 | bytes 1572864 | tf_op jit(solution)/shard_map/pallas_call | solution.py:338
  69.3 1.9 %shard_map.114.part_ref = f32[256,256]{1,0:T(8,128)S(1)} custom-call(f32[8,256,256]{2,1,0:T(8,128)} %left.15, f32[8,512,256]{2,1,0:T(8,128)} %right.15, f32[384,256]{1,0:T(8,128)S(1)} %collective-permute-done.12.refs_0_, f32[384,256]{1,0:T(8,128)S(1)} %collective-permute-done.13.refs_1_, f32[384,256]{1,0:T(8,128)S(1)} %collective-permute-done.14.refs_2_, ...), custom_call_target="tpu_custom_call" | custom-call | flops 402653184 | bytes 1572864 | tf_op jit(solution)/shard_map/pallas_call | solution.py:338
  71.2 1.9 %shard_map.108.part_ref = f32[256,256]{1,0:T(8,128)S(1)} custom-call(f32[8,256,256]{2,1,0:T(8,128)} %left.15, f32[8,512,256]{2,1,0:T(8,128)} %right.15, f32[384,256]{1,0:T(8,128)S(1)} %collective-permute-done.refs_0_, f32[384,256]{1,0:T(8,128)S(1)} %collective-permute-done.1.refs_1_, f32[384,256]{1,0:T(8,128)S(1)} %collective-permute-done.2.refs_2_, ...), custom_call_target="tpu_custom_call" | custom-call | flops 402653184 | bytes 1572864 | tf_op jit(solution)/shard_map/pallas_call | solution.py:338
  75.8 5.4 %collective-permute-start.21 = (f32[256,256]{1,0:T(8,128)}, f32[256,256]{1,0:T(8,128)}, u32[]{:S(2)}, u32[]{:S(2)}) collective-permute-start(f32[256,256]{1,0:T(8,128)} %shard_map.118.refs_10_), channel_id=1, source_target_pairs={{0,128},{32,160},{64,192},{96,224},{128,0},{160,32},{192,64},{224,... | collective-permute-start | bytes 786440 | tf_op jit(solution)/shard_map/ppermute | solution.py:310
  81.2 5.0 %collective-permute-done.9.down = f32[256,512]{1,0:T(8,128)S(1)} collective-permute-done((f32[256,512]{1,0:T(8,128)S(1)}, f32[256,512]{1,0:T(8,128)S(1)}, u32[]{:S(2)}, u32[]{:S(2)}) %collective-permute-start.9) | collective-permute-done | bytes 524320 | tf_op jit(solution)/shard_map/ppermute | solution.py:310
  86.3 4.2 %collective-permute-start.16 = (f32[256,256]{1,0:T(8,128)}, f32[256,256]{1,0:T(8,128)}, u32[]{:S(2)}, u32[]{:S(2)}) collective-permute-start(f32[256,256]{1,0:T(8,128)} %shard_map.115.refs_9_), channel_id=1, source_target_pairs={{0,128},{32,160},{64,192},{96,224},{128,0},{160,32},{192,64},{224,... | collective-permute-start | bytes 786440 | tf_op jit(solution)/shard_map/ppermute | solution.py:310
  94.5 1.9 %shard_map.111.part_ref = f32[256,256]{1,0:T(8,128)S(1)} custom-call(f32[8,256,256]{2,1,0:T(8,128)} %left.15, f32[8,512,256]{2,1,0:T(8,128)} %right.15, f32[384,256]{1,0:T(8,128)S(1)} %collective-permute-done.refs_0_, f32[384,256]{1,0:T(8,128)S(1)} %collective-permute-done.1.refs_1_, f32[384,256]{1,0:T(8,128)S(1)} %collective-permute-done.2.refs_2_, ...), custom_call_target="tpu_custom_call" | custom-call | flops 402653184 | bytes 1572864 | tf_op jit(solution)/shard_map/pallas_call | solution.py:338
  96.9 4.0 %collective-permute-start.22 = (f32[264,256]{1,0:T(8,128)S(1)}, f32[264,256]{1,0:T(8,128)S(1)}, u32[]{:S(2)}, u32[]{:S(2)}) collective-permute-start(f32[264,256]{1,0:T(8,128)S(1)} %shard_map.112.refs_9_), channel_id=1, source_target_pairs={{0,128},{32,160},{64,192},{96,224},{128,0},{160,32},{192,64},{224,... | collective-permute-start | bytes 811016 | tf_op jit(solution)/shard_map/ppermute | solution.py:310
  100.9 2.6 %collective-permute-done.16.refs_10_ = f32[256,256]{1,0:T(8,128)} collective-permute-done((f32[256,256]{1,0:T(8,128)}, f32[256,256]{1,0:T(8,128)}, u32[]{:S(2)}, u32[]{:S(2)}) %collective-permute-start.16) | collective-permute-done | bytes 262176 | tf_op jit(solution)/shard_map/ppermute | solution.py:310
  103.5 4.8 %shard_map.119 = (f32[256,512]{1,0:T(8,128)}, f32[4,256]{1,0:T(4,128)S(1)}) custom-call(f32[8,256,256]{2,1,0:T(8,128)} %left.15, f32[8,512,256]{2,1,0:T(8,128)} %right.15, f32[384,256]{1,0:T(8,128)} %copy-done, f32[384,256]{1,0:T(8,128)} %copy-done.1, f32[384,256]{1,0:T(8,128)} %copy-done.2, f32[128,256]{1,0:T(8,128)} %copy-done.15, f32[128,256]{1,0:T(8,128)} %copy-done.16, ...), custom_call_target="tpu_custom_call" | custom-call | flops 402653184 | bytes 1572864 | tf_op jit(solution)/shard_map/pallas_call | solution.py:338
  109.6 3.1 %shard_map.120 = (f32[4,256]{1,0:T(4,128)S(1)}, bf16[4,256,256]{2,1,0:T(8,128)(2,1)S(1)}, bf16[4,256,256]{2,1,0:T(8,128)(2,1)S(1)}, f32[256,256]{1,0:T(8,128)S(1...) custom-call(f32[8,256,256]{2,1,0:T(8,128)} %left.15, f32[8,512,256]{2,1,0:T(8,128)} %right.15, ...), custom_call_target="tpu_custom_call" | custom-call | flops 402653184 | bytes 1572864 | tf_op jit(solution)/shard_map/pallas_call | solution.py:424
  112.7 2.9 %collective-permute-done.22.block = f32[264,256]{1,0:T(8,128)S(1)} collective-permute-done((f32[264,256]{1,0:T(8,128)S(1)}, f32[264,256]{1,0:T(8,128)S(1)}, u32[]{:S(2)}, u32[]{:S(2)}) %collective-permute-start.22) | collective-permute-done | bytes 270368 | tf_op jit(solution)/shard_map/ppermute | solution.py:310
  118.1 20.6 %collective-permute-start.26 = (f32[2,256]{1,0:T(2,128)S(1)}, f32[2,256]{1,0:T(2,128)S(1)}, u32[]{:S(2)}, u32[]{:S(2)}) collective-permute-start(f32[2,256]{1,0:T(2,128)S(1)} %bitcast.33), channel_id=1, source_target_pairs={{0,64},{32,96},{64,0},{96,32},{128,192},{160,224},{192,128},{224,1... | collective-permute-start | bytes 6152 | tf_op jit(solution)/shard_map/ppermute | solution.py:443
  (104 shorter events, 28.1 us)
Async XLA Ops:
  3.3 6.9 %collective-permute-start.17 = (f32[128,256]{1,0:T(8,128)S(1)}, f32[128,256]{1,0:T(8,128)S(1)}, u32[]{:S(2)}, u32[]{:S(2)}) collective-permute-start(f32[128,256]{1,0:T(8,128)S(1)} %get-tuple-element.35), channel_id=1, source_target_pairs={{0,32},{32,64},{64,96},{96,0},{128,160},{160,192},{192,224},{224,1... | collective-permute-start | bytes 393224 | tf_op jit(solution)/shard_map/ppermute | solution.py:310
  5.4 9.2 %collective-permute-start.18 = (f32[128,256]{1,0:T(8,128)S(1)}, f32[128,256]{1,0:T(8,128)S(1)}, u32[]{:S(2)}, u32[]{:S(2)}) collective-permute-start(f32[128,256]{1,0:T(8,128)S(1)} %get-tuple-element.36), channel_id=1, source_target_pairs={{0,64},{32,96},{64,0},{96,32},{128,192},{160,224},{192,128},{224,1... | collective-permute-start | bytes 393224 | tf_op jit(solution)/shard_map/ppermute | solution.py:310
  7.8 7.3 %collective-permute-start.19 = (f32[128,256]{1,0:T(8,128)S(1)}, f32[128,256]{1,0:T(8,128)S(1)}, u32[]{:S(2)}, u32[]{:S(2)}) collective-permute-start(f32[128,256]{1,0:T(8,128)S(1)} %get-tuple-element.37), channel_id=1, source_target_pairs={{0,96},{32,0},{64,32},{96,64},{128,224},{160,128},{192,160},{224,1... | collective-permute-start | bytes 393224 | tf_op jit(solution)/shard_map/ppermute | solution.py:310
  9.0 32.9 %collective-permute-start.12 = (f32[384,256]{1,0:T(8,128)S(1)}, f32[384,256]{1,0:T(8,128)S(1)}, u32[]{:S(2)}, u32[]{:S(2)}) collective-permute-start(f32[384,256]{1,0:T(8,128)S(1)} %get-tuple-element.32), channel_id=1, source_target_pairs={{0,32},{32,64},{64,96},{96,0},{128,160},{160,192},{192,224},{224,1... | collective-permute-start | bytes 1179656 | tf_op jit(solution)/shard_map/ppermute | solution.py:310
  9.3 33.8 %collective-permute-start.13 = (f32[384,256]{1,0:T(8,128)S(1)}, f32[384,256]{1,0:T(8,128)S(1)}, u32[]{:S(2)}, u32[]{:S(2)}) collective-permute-start(f32[384,256]{1,0:T(8,128)S(1)} %get-tuple-element.33), channel_id=1, source_target_pairs={{0,64},{32,96},{64,0},{96,32},{128,192},{160,224},{192,128},{224,1... | collective-permute-start | bytes 1179656 | tf_op jit(solution)/shard_map/ppermute | solution.py:310
  10.2 36.9 %collective-permute-start.14 = (f32[384,256]{1,0:T(8,128)S(1)}, f32[384,256]{1,0:T(8,128)S(1)}, u32[]{:S(2)}, u32[]{:S(2)}) collective-permute-start(f32[384,256]{1,0:T(8,128)S(1)} %get-tuple-element.34), channel_id=1, source_target_pairs={{0,96},{32,0},{64,32},{96,64},{128,224},{160,128},{192,160},{224,1... | collective-permute-start | bytes 1179656 | tf_op jit(solution)/shard_map/ppermute | solution.py:310
  14.6 20.7 %collective-permute-start.3 = (f32[128,256]{1,0:T(8,128)S(1)}, f32[128,256]{1,0:T(8,128)S(1)}, u32[]{:S(2)}, u32[]{:S(2)}) collective-permute-start(f32[128,256]{1,0:T(8,128)S(1)} %get-tuple-element.28), channel_id=1, source_target_pairs={{0,32},{32,64},{64,96},{96,0},{128,160},{160,192},{192,224},{224,1... | collective-permute-start | bytes 393224 | tf_op jit(solution)/shard_map/ppermute | solution.py:310
  15.2 20.9 %collective-permute-start.4 = (f32[128,256]{1,0:T(8,128)S(1)}, f32[128,256]{1,0:T(8,128)S(1)}, u32[]{:S(2)}, u32[]{:S(2)}) collective-permute-start(f32[128,256]{1,0:T(8,128)S(1)} %get-tuple-element.29), channel_id=1, source_target_pairs={{0,64},{32,96},{64,0},{96,32},{128,192},{160,224},{192,128},{224,1... | collective-permute-start | bytes 393224 | tf_op jit(solution)/shard_map/ppermute | solution.py:310
  35.3 13.0 %collective-permute-start = (f32[384,256]{1,0:T(8,128)S(1)}, f32[384,256]{1,0:T(8,128)S(1)}, u32[]{:S(2)}, u32[]{:S(2)}) collective-permute-start(f32[384,256]{1,0:T(8,128)S(1)} %get-tuple-element.25), channel_id=1, source_target_pairs={{0,32},{32,64},{64,96},{96,0},{128,160},{160,192},{192,224},{224,1... | collective-permute-start | bytes 1179656 | tf_op jit(solution)/shard_map/ppermute | solution.py:310
  40.0 16.5 %collective-permute-start.1 = (f32[384,256]{1,0:T(8,128)S(1)}, f32[384,256]{1,0:T(8,128)S(1)}, u32[]{:S(2)}, u32[]{:S(2)}) collective-permute-start(f32[384,256]{1,0:T(8,128)S(1)} %get-tuple-element.26), channel_id=1, source_target_pairs={{0,64},{32,96},{64,0},{96,32},{128,192},{160,224},{192,128},{224,1... | collective-permute-start | bytes 1179656 | tf_op jit(solution)/shard_map/ppermute | solution.py:310
  41.8 21.9 %collective-permute-start.2 = (f32[384,256]{1,0:T(8,128)S(1)}, f32[384,256]{1,0:T(8,128)S(1)}, u32[]{:S(2)}, u32[]{:S(2)}) collective-permute-start(f32[384,256]{1,0:T(8,128)S(1)} %get-tuple-element.27), channel_id=1, source_target_pairs={{0,96},{32,0},{64,32},{96,64},{128,224},{160,128},{192,160},{224,1... | collective-permute-start | bytes 1179656 | tf_op jit(solution)/shard_map/ppermute | solution.py:310
  43.1 22.0 %collective-permute-start.20 = (f32[3,128,256]{2,1,0:T(8,128)S(1)}, f32[3,128,256]{2,1,0:T(8,128)S(1)}, u32[]{:S(2)}, u32[]{:S(2)}) collective-permute-start(f32[3,128,256]{2,1,0:T(8,128)S(1)} %shard_map.116.refs_3_), channel_id=1, source_target_pairs={{0,1},{1,0},{2,3},{3,2},{4,5},{5,4},{6,7},{7,6},{8,9},{9,8},{10,11... | collective-permute-start | bytes 1179656 | tf_op jit(solution)/shard_map/ppermute | solution.py:310
  47.1 19.4 %collective-permute-start.11 = (f32[256,512]{1,0:T(8,128)S(1)}, f32[256,512]{1,0:T(8,128)S(1)}, u32[]{:S(2)}, u32[]{:S(2)}) collective-permute-start(f32[256,512]{1,0:T(8,128)S(1)} %get-tuple-element.24._.mixed), channel_id=1, source_target_pairs={{16,0},{18,2},{20,4},{22,6},{24,8},{26,10},{28,12},{30,14},{0,16},... | collective-permute-start | bytes 1572872 | tf_op jit(solution)/shard_map/ppermute | solution.py:310
  48.4 18.6 %collective-permute-start.15 = (f32[3,128,256]{2,1,0:T(8,128)S(1)}, f32[3,128,256]{2,1,0:T(8,128)S(1)}, u32[]{:S(2)}, u32[]{:S(2)}) collective-permute-start(f32[3,128,256]{2,1,0:T(8,128)S(1)} %shard_map.113.refs_3_), channel_id=1, source_target_pairs={{0,1},{1,0},{2,3},{3,2},{4,5},{5,4},{6,7},{7,6},{8,9},{9,8},{10,11... | collective-permute-start | bytes 1179656 | tf_op jit(solution)/shard_map/ppermute | solution.py:310
  56.5 19.3 %collective-permute-start.10 = (f32[256,512]{1,0:T(8,128)S(1)}, f32[256,512]{1,0:T(8,128)S(1)}, u32[]{:S(2)}, u32[]{:S(2)}) collective-permute-start(f32[256,512]{1,0:T(8,128)S(1)} %get-tuple-element.24._.mixed), channel_id=1, source_target_pairs={{8,6},{16,14},{24,22},{0,30},{30,0},{6,8},{14,16},{22,24},{9,7},{1... | collective-permute-start | bytes 1572872 | tf_op jit(solution)/shard_map/ppermute | solution.py:310
  63.8 22.5 %collective-permute-start.9 = (f32[256,512]{1,0:T(8,128)S(1)}, f32[256,512]{1,0:T(8,128)S(1)}, u32[]{:S(2)}, u32[]{:S(2)}) collective-permute-start(f32[256,512]{1,0:T(8,128)S(1)} %get-tuple-element.24._.mixed), channel_id=1, source_target_pairs={{0,2},{2,4},{4,6},{8,10},{10,12},{12,14},{16,18},{18,20},{20,22},{... | collective-permute-start | bytes 1572872 | tf_op jit(solution)/shard_map/ppermute | solution.py:310
  65.1 25.3 %collective-permute-start.8 = (f32[256,512]{1,0:T(8,128)S(1)}, f32[256,512]{1,0:T(8,128)S(1)}, u32[]{:S(2)}, u32[]{:S(2)}) collective-permute-start(f32[256,512]{1,0:T(8,128)S(1)} %get-tuple-element.24._.mixed), channel_id=1, source_target_pairs={{2,0},{4,2},{6,4},{10,8},{12,10},{14,12},{18,16},{20,18},{22,20},{... | collective-permute-start | bytes 1572872 | tf_op jit(solution)/shard_map/ppermute | solution.py:310
  66.5 25.2 %collective-permute-start.6 = (f32[3,128,256]{2,1,0:T(8,128)S(1)}, f32[3,128,256]{2,1,0:T(8,128)S(1)}, u32[]{:S(2)}, u32[]{:S(2)}) collective-permute-start(f32[3,128,256]{2,1,0:T(8,128)S(1)} %shard_map.106.refs_3_), channel_id=1, source_target_pairs={{0,1},{1,0},{2,3},{3,2},{4,5},{5,4},{6,7},{7,6},{8,9},{9,8},{10,11... | collective-permute-start | bytes 1179656 | tf_op jit(solution)/shard_map/ppermute | solution.py:310
  67.0 29.4 %collective-permute-start.7 = (f32[3,128,256]{2,1,0:T(8,128)S(1)}, f32[3,128,256]{2,1,0:T(8,128)S(1)}, u32[]{:S(2)}, u32[]{:S(2)}) collective-permute-start(f32[3,128,256]{2,1,0:T(8,128)S(1)} %shard_map.107.refs_3_), channel_id=1, source_target_pairs={{0,1},{1,0},{2,3},{3,2},{4,5},{5,4},{6,7},{7,6},{8,9},{9,8},{10,11... | collective-permute-start | bytes 1179656 | tf_op jit(solution)/shard_map/ppermute | solution.py:310
  75.8 25.1 %collective-permute-start.21 = (f32[256,256]{1,0:T(8,128)}, f32[256,256]{1,0:T(8,128)}, u32[]{:S(2)}, u32[]{:S(2)}) collective-permute-start(f32[256,256]{1,0:T(8,128)} %shard_map.118.refs_10_), channel_id=1, source_target_pairs={{0,128},{32,160},{64,192},{96,224},{128,0},{160,32},{192,64},{224,... | collective-permute-start | bytes 786440 | tf_op jit(solution)/shard_map/ppermute | solution.py:310
  86.3 17.2 %collective-permute-start.16 = (f32[256,256]{1,0:T(8,128)}, f32[256,256]{1,0:T(8,128)}, u32[]{:S(2)}, u32[]{:S(2)}) collective-permute-start(f32[256,256]{1,0:T(8,128)} %shard_map.115.refs_9_), channel_id=1, source_target_pairs={{0,128},{32,160},{64,192},{96,224},{128,0},{160,32},{192,64},{224,... | collective-permute-start | bytes 786440 | tf_op jit(solution)/shard_map/ppermute | solution.py:310
  93.0 16.6 %collective-permute-start.23 = (f32[264,256]{1,0:T(8,128)}, f32[264,256]{1,0:T(8,128)}, u32[]{:S(2)}, u32[]{:S(2)}) collective-permute-start(f32[264,256]{1,0:T(8,128)} %shard_map.110.refs_8_), channel_id=1, source_target_pairs={{0,128},{32,160},{64,192},{96,224},{128,0},{160,32},{192,64},{224,... | collective-permute-start | bytes 811016 | tf_op jit(solution)/shard_map/ppermute | solution.py:310
  96.9 18.7 %collective-permute-start.22 = (f32[264,256]{1,0:T(8,128)S(1)}, f32[264,256]{1,0:T(8,128)S(1)}, u32[]{:S(2)}, u32[]{:S(2)}) collective-permute-start(f32[264,256]{1,0:T(8,128)S(1)} %shard_map.112.refs_9_), channel_id=1, source_target_pairs={{0,128},{32,160},{64,192},{96,224},{128,0},{160,32},{192,64},{224,... | collective-permute-start | bytes 811016 | tf_op jit(solution)/shard_map/ppermute | solution.py:310
  118.1 22.1 %collective-permute-start.26 = (f32[2,256]{1,0:T(2,128)S(1)}, f32[2,256]{1,0:T(2,128)S(1)}, u32[]{:S(2)}, u32[]{:S(2)}) collective-permute-start(f32[2,256]{1,0:T(2,128)S(1)} %bitcast.33), channel_id=1, source_target_pairs={{0,64},{32,96},{64,0},{96,32},{128,192},{160,224},{192,128},{224,1... | collective-permute-start | bytes 6152 | tf_op jit(solution)/shard_map/ppermute | solution.py:443
  (25 other events, 504.7 us)

commit v2 on v1

--- a/solution.py
+++ b/solution.py
@@ -15,7 +15,6 @@
 SCALARS = pl.BlockSpec(memory_space=pltpu.SMEM)
 WHOLE = pl.BlockSpec(memory_space=pltpu.VMEM)
 LIMIT = pltpu.CompilerParams(vmem_limit_bytes=16 << 20)
-SEGMENT = 4
 EXTRA = 8
 
 
@@ -261,7 +260,7 @@
         sums_ref[spot : spot + 1, :] = before[spot : spot + 1, :] + jnp.sum(long[0:rows, :] * product, axis=0, keepdims=True)
 
 
-def correction_kernel(pairs_per_shard, shards, neighbours, coupling, mixed, up, down, wrap, far, d_ref, out_ref):
+def correction_kernel(pairs_per_shard, shards, neighbours, coupling, mixed, first, second, far, d_ref, out_ref):
     shard = lax.axis_index("pair")
 
     def weight(by):
@@ -272,11 +271,19 @@
         return total
 
     above, below = weight(1), weight(shards - 1)
-    spot = shard % SEGMENT
-    ends = jnp.where(spot == SEGMENT - 1, above, jnp.where(spot == 0, below, 0.0))
-    total = weight(0) * mixed[...] + above * up[...] + below * down[...]
-    total += ends * wrap[...] + weight(shards // 2) * far[...]
+    even = shard % 2 == 0
+    total = weight(0) * mixed[...] + jnp.where(even, above, below) * first[...]
+    total += jnp.where(even, below, above) * second[...] + weight(shards // 2) * far[...]
     out_ref[...] = dot3(halves(total), halves(d_ref[...]), NN)
+
+
+def seat_kernel(ring, *refs):
+    *parts, out_ref = refs
+    place, first = seat(ring, True)
+    for by, part in enumerate(parts):
+        at = (place + by) % ring
+        out_ref[pl.ds(first + at, 1), :] = part[0:1, :]
+        out_ref[pl.ds(ring - first + at, 1), :] = part[1:2, :]
 
 
 def vmem(*arrays):
@@ -295,8 +302,6 @@
     fit_count, pair_count = lax.axis_size("fit"), lax.axis_size("pair")
     ring = fit_count // 2
     rows, width, depth = left.shape[1], right.shape[1], left.shape[2]
-    fit = lax.axis_index("fit")
-    side, place = fit // ring, fit % ring
     amp, trans = amplitudes[0], domain_trans[0]
     swap = [(0, 1), (1, 0)]
     across = [(f, (f + ring) % fit_count) for f in range(fit_count)]
@@ -362,9 +367,8 @@
     their_longs, their_shorts = spread(sent[: ring - 1]), spread(sent[ring - 1 :])
     shards = range(pair_count)
     near = [
-        from_shards(mixed, [(s, s + 1) for s in shards if s % SEGMENT < SEGMENT - 1]),
-        from_shards(mixed, [(s, s - 1) for s in shards if s % SEGMENT > 0]),
-        from_shards(mixed, [(s, s + 1) for s in shards if s % SEGMENT == SEGMENT - 1] + [(s, s - 1) for s in shards if s % SEGMENT == 0]),
+        from_shards(mixed, [(s, s + 1 - 2 * (s % 2)) for s in shards]),
+        from_shards(mixed, [(s, s - 1 + 2 * (s % 2)) for s in shards]),
         from_shards(mixed, [(s, s + pair_count // 2) for s in shards]),
     ]
     *sent, facts = pl.pallas_call(
@@ -379,7 +383,7 @@
     my_longs, my_shorts = spread(sent[: ring - 1]), spread(sent[ring - 1 :])
     (corr,) = pl.pallas_call(
         functools.partial(correction_kernel, fit_count, pair_count),
-        in_specs=[SCALARS] * 2 + [WHOLE] * 6,
+        in_specs=[SCALARS] * 2 + [WHOLE] * 5,
         out_specs=[WHOLE],
         out_shape=[block],
         compiler_params=LIMIT,
@@ -441,12 +445,15 @@
     both = jnp.stack([my_sums, their_sums], axis=1)
     both = both + lax.ppermute(both, "blk", swap)
     parts = [both[0]] + [lax.ppermute(both[by], "fit", shifted(-by)) for by in range(1, ring)]
-    density = jnp.zeros((2, ring, depth), F32)
-    for by, part in enumerate(parts):
-        at = (place + by) % ring
-        density = jnp.where((jnp.arange(ring) == at)[None, :, None], part[:, None, :], density)
-    density = jnp.where(side == 0, density, density[::-1])
-    return new[None], density.reshape(fit_count, depth)
+    density = pl.pallas_call(
+        functools.partial(seat_kernel, ring),
+        in_specs=[WHOLE] * ring,
+        out_specs=WHOLE,
+        out_shape=jax.ShapeDtypeStruct((fit_count, depth), F32),
+        compiler_params=LIMIT,
+        cost_estimate=cost(0, 8 * fit_count * depth),
+    )(*parts)
+    return new[None], density
 
 
 def solution(mesh):

time: 144 us -> 157 us (1.090)
  the two profiles are of different devices: /device:TPU:1 before, /device:TPU:48 now
where the time goes in v2:
time: 157 us
  waiting for transfers between devices  78 us (50%)
  starting transfers between devices  54.8 us (35%)
  Pallas kernels  21.8 us (14%)
  between operations  2.35 us (1%)
    ppermute x23, waiting for transfers between devices, send(): return lax.ppermute(value, axis, pairs)  73.3 us
    ppermute x23, starting transfers between devices, send(): return lax.ppermute(value, axis, pairs)  50.7 us
    pallas_call x5, Pallas kernels, work(): pl.pallas_call(functools.partial(kernel, ring, own, which), in_specs=[ANY...  11.1 us
    ppermute x3, starting transfers between devices, body(): lax.ppermute(both[by], 'fit', shifted(-by))  4.03 us
    ppermute x3, waiting for transfers between devices, body(): lax.ppermute(both[by], 'fit', shifted(-by))  3.47 us
  transfers between devices with their start and end apart: 27, of which 9 were waited for; matrix products, arithmetic and copies ran while one was open for 0% of the time, Pallas kernels for 11%

profile of v2, /device:TPU:48, one launch (start us, length us, event | category | flops | bytes accessed | tf_op | source)
XLA Modules:
  0.0 157.0 jit_solution(8281838850230494346)
XLA Ops:
  0.6 2.6 %shard_map.104 = (f32[384,256]{1,0:T(8,128)S(1)}, f32[384,256]{1,0:T(8,128)S(1)}, f32[384,256]{1,0:T(8,128)S(1)}, f32[128,256]{1,0:T(8,128)S(1)}, f32[128,256]{1...) custom-call(f32[8,256,256]{2,1,0:T(8,128)} %left.15, f32[8,512,256]{2,1,0:T(8,128)} %right.15, ...), custom_call_target="tpu_custom_call" | custom-call | flops 402653184 | bytes 4194304 | tf_op jit(solution)/shard_map/pallas_call | solution.py:358
  9.2 1.7 %collective-permute-start.12 = (f32[384,256]{1,0:T(8,128)S(1)}, f32[384,256]{1,0:T(8,128)S(1)}, u32[]{:S(2)}, u32[]{:S(2)}) collective-permute-start(f32[384,256]{1,0:T(8,128)S(1)} %get-tuple-element.33), channel_id=1, source_target_pairs={{0,64},{32,96},{64,0},{96,32},{128,192},{160,224},{192,128},{224,1... | collective-permute-start | bytes 1179656 | tf_op jit(solution)/shard_map/ppermute | solution.py:315
  10.9 1.8 %collective-permute-start.4 = (f32[128,256]{1,0:T(8,128)S(1)}, f32[128,256]{1,0:T(8,128)S(1)}, u32[]{:S(2)}, u32[]{:S(2)}) collective-permute-start(f32[128,256]{1,0:T(8,128)S(1)} %get-tuple-element.29), channel_id=1, source_target_pairs={{0,64},{32,96},{64,0},{96,32},{128,192},{160,224},{192,128},{224,1... | collective-permute-start | bytes 393224 | tf_op jit(solution)/shard_map/ppermute | solution.py:315
  13.9 15.6 %collective-permute-done.3.refs_0_.refs_3_ = f32[128,256]{1,0:T(8,128)S(1)} collective-permute-done((f32[128,256]{1,0:T(8,128)S(1)}, f32[128,256]{1,0:T(8,128)S(1)}, u32[]{:S(2)}, u32[]{:S(2)}) %collective-permute-start.3) | collective-permute-done | bytes 131104 | tf_op jit(solution)/shard_map/ppermute | solution.py:315
  29.6 2.1 %collective-permute-done.4.refs_1_.refs_4_ = f32[128,256]{1,0:T(8,128)S(1)} collective-permute-done((f32[128,256]{1,0:T(8,128)S(1)}, f32[128,256]{1,0:T(8,128)S(1)}, u32[]{:S(2)}, u32[]{:S(2)}) %collective-permute-start.4) | collective-permute-done | bytes 131104 | tf_op jit(solution)/shard_map/ppermute | solution.py:315
  32.5 1.8 %collective-permute-start.18 = (f32[128,256]{1,0:T(8,128)S(1)}, f32[128,256]{1,0:T(8,128)S(1)}, u32[]{:S(2)}, u32[]{:S(2)}) collective-permute-start(f32[128,256]{1,0:T(8,128)S(1)} %get-tuple-element.37), channel_id=1, source_target_pairs={{0,96},{32,0},{64,32},{96,64},{128,224},{160,128},{192,160},{224,1... | collective-permute-start | bytes 393224 | tf_op jit(solution)/shard_map/ppermute | solution.py:315
  34.3 5.2 %collective-permute-done.17.refs_1_.refs_4_ = f32[128,256]{1,0:T(8,128)S(1)} collective-permute-done((f32[128,256]{1,0:T(8,128)S(1)}, f32[128,256]{1,0:T(8,128)S(1)}, u32[]{:S(2)}, u32[]{:S(2)}) %collective-permute-start.17) | collective-permute-done | bytes 131104 | tf_op jit(solution)/shard_map/ppermute | solution.py:315
  39.5 3.5 %collective-permute-start = (f32[384,256]{1,0:T(8,128)S(1)}, f32[384,256]{1,0:T(8,128)S(1)}, u32[]{:S(2)}, u32[]{:S(2)}) collective-permute-start(f32[384,256]{1,0:T(8,128)S(1)} %get-tuple-element.25), channel_id=1, source_target_pairs={{0,32},{32,64},{64,96},{96,0},{128,160},{160,192},{192,224},{224,1... | collective-permute-start | bytes 1179656 | tf_op jit(solution)/shard_map/ppermute | solution.py:315
  43.0 3.4 %collective-permute-start.1 = (f32[384,256]{1,0:T(8,128)S(1)}, f32[384,256]{1,0:T(8,128)S(1)}, u32[]{:S(2)}, u32[]{:S(2)}) collective-permute-start(f32[384,256]{1,0:T(8,128)S(1)} %get-tuple-element.26), channel_id=1, source_target_pairs={{0,64},{32,96},{64,0},{96,32},{128,192},{160,224},{192,128},{224,1... | collective-permute-start | bytes 1179656 | tf_op jit(solution)/shard_map/ppermute | solution.py:315
  47.3 14.0 %collective-permute-done.5.refs_2_.refs_5_ = f32[128,256]{1,0:T(8,128)S(1)} collective-permute-done((f32[128,256]{1,0:T(8,128)S(1)}, f32[128,256]{1,0:T(8,128)S(1)}, u32[]{:S(2)}, u32[]{:S(2)}) %collective-permute-start.5) | collective-permute-done | bytes 131104 | tf_op jit(solution)/shard_map/ppermute | solution.py:315
  61.5 3.7 %collective-permute-start.9 = (f32[256,512]{1,0:T(8,128)S(1)}, f32[256,512]{1,0:T(8,128)S(1)}, u32[]{:S(2)}, u32[]{:S(2)}) collective-permute-start(f32[256,512]{1,0:T(8,128)S(1)} %get-tuple-element.24._.mixed), channel_id=1, source_target_pairs={{30,0},{4,2},{2,4},{8,6},{6,8},{12,10},{10,12},{16,14},{14,16},{20... | collective-permute-start | bytes 1572872 | tf_op jit(solution)/shard_map/ppermute | solution.py:315
  66.5 1.9 %shard_map.108.part_ref = f32[256,256]{1,0:T(8,128)S(1)} custom-call(f32[8,256,256]{2,1,0:T(8,128)} %left.15, f32[8,512,256]{2,1,0:T(8,128)} %right.15, f32[384,256]{1,0:T(8,128)S(1)} %collective-permute-done.refs_0_, f32[384,256]{1,0:T(8,128)S(1)} %collective-permute-done.1.refs_1_, f32[384,256]{1,0:T(8,128)S(1)} %collective-permute-done.2.refs_2_, ...), custom_call_target="tpu_custom_call" | custom-call | flops 402653184 | bytes 1572864 | tf_op jit(solution)/shard_map/pallas_call | solution.py:343
  68.4 1.9 %shard_map.114.part_ref = f32[256,256]{1,0:T(8,128)S(1)} custom-call(f32[8,256,256]{2,1,0:T(8,128)} %left.15, f32[8,512,256]{2,1,0:T(8,128)} %right.15, f32[384,256]{1,0:T(8,128)S(1)} %collective-permute-done.11.refs_0_, f32[384,256]{1,0:T(8,128)S(1)} %collective-permute-done.12.refs_1_, f32[384,256]{1,0:T(8,128)S(1)} %collective-permute-done.13.refs_2_, ...), custom_call_target="tpu_custom_call" | custom-call | flops 402653184 | bytes 1572864 | tf_op jit(solution)/shard_map/pallas_call | solution.py:343
  70.3 1.9 %shard_map.117.part_ref = f32[256,256]{1,0:T(8,128)S(1)} custom-call(f32[8,256,256]{2,1,0:T(8,128)} %left.15, f32[8,512,256]{2,1,0:T(8,128)} %right.15, f32[384,256]{1,0:T(8,128)S(1)} %collective-permute-done.11.refs_0_, f32[384,256]{1,0:T(8,128)S(1)} %collective-permute-done.12.refs_1_, f32[384,256]{1,0:T(8,128)S(1)} %collective-permute-done.13.refs_2_, ...), custom_call_target="tpu_custom_call" | custom-call | flops 402653184 | bytes 1572864 | tf_op jit(solution)/shard_map/pallas_call | solution.py:343
  73.2 2.9 %collective-permute-done.8.first = f32[256,512]{1,0:T(8,128)S(1)} collective-permute-done((f32[256,512]{1,0:T(8,128)S(1)}, f32[256,512]{1,0:T(8,128)S(1)}, u32[]{:S(2)}, u32[]{:S(2)}) %collective-permute-start.8) | collective-permute-done | bytes 524320 | tf_op jit(solution)/shard_map/ppermute | solution.py:315
  76.2 6.3 %collective-permute-start.20 = (f32[256,256]{1,0:T(8,128)S(1)}, f32[256,256]{1,0:T(8,128)S(1)}, u32[]{:S(2)}, u32[]{:S(2)}) collective-permute-start(f32[256,256]{1,0:T(8,128)S(1)} %shard_map.118.refs_10_), channel_id=1, source_target_pairs={{0,128},{32,160},{64,192},{96,224},{128,0},{160,32},{192,64},{224,... | collective-permute-start | bytes 786440 | tf_op jit(solution)/shard_map/ppermute | solution.py:315
  82.5 33.4 %collective-permute-done.9.second = f32[256,512]{1,0:T(8,128)S(1)} collective-permute-done((f32[256,512]{1,0:T(8,128)S(1)}, f32[256,512]{1,0:T(8,128)S(1)}, u32[]{:S(2)}, u32[]{:S(2)}) %collective-permute-start.9) | collective-permute-done | bytes 524320 | tf_op jit(solution)/shard_map/ppermute | solution.py:315
  115.9 15.0 %collective-permute-start.15 = (f32[256,256]{1,0:T(8,128)S(1)}, f32[256,256]{1,0:T(8,128)S(1)}, u32[]{:S(2)}, u32[]{:S(2)}) collective-permute-start(f32[256,256]{1,0:T(8,128)S(1)} %shard_map.115.refs_9_), channel_id=1, source_target_pairs={{0,128},{32,160},{64,192},{96,224},{128,0},{160,32},{192,64},{224,... | collective-permute-start | bytes 786440 | tf_op jit(solution)/shard_map/ppermute | solution.py:315
  132.8 1.9 %shard_map.111.part_ref = f32[256,256]{1,0:T(8,128)S(1)} custom-call(f32[8,256,256]{2,1,0:T(8,128)} %left.15, f32[8,512,256]{2,1,0:T(8,128)} %right.15, f32[384,256]{1,0:T(8,128)S(1)} %collective-permute-done.refs_0_, f32[384,256]{1,0:T(8,128)S(1)} %collective-permute-done.1.refs_1_, f32[384,256]{1,0:T(8,128)S(1)} %collective-permute-done.2.refs_2_, ...), custom_call_target="tpu_custom_call" | custom-call | flops 402653184 | bytes 1572864 | tf_op jit(solution)/shard_map/pallas_call | solution.py:343
  135.3 6.0 %collective-permute-start.21 = (f32[264,256]{1,0:T(8,128)S(1)}, f32[264,256]{1,0:T(8,128)S(1)}, u32[]{:S(2)}, u32[]{:S(2)}) collective-permute-start(f32[264,256]{1,0:T(8,128)S(1)} %shard_map.112.refs_9_), channel_id=1, source_target_pairs={{0,128},{32,160},{64,192},{96,224},{128,0},{160,32},{192,64},{224,... | collective-permute-start | bytes 811016 | tf_op jit(solution)/shard_map/ppermute | solution.py:315
  141.3 3.6 %shard_map.119 = (f32[256,512]{1,0:T(8,128)}, f32[4,256]{1,0:T(4,128)S(1)}) custom-call(f32[8,256,256]{2,1,0:T(8,128)} %left.15, f32[8,512,256]{2,1,0:T(8,128)} %right.15, f32[384,256]{1,0:T(8,128)} %copy-done, f32[384,256]{1,0:T(8,128)} %copy-done.1, f32[384,256]{1,0:T(8,128)} %copy-done.2, f32[128,256]{1,0:T(8,128)} %copy-done.7, f32[128,256]{1,0:T(8,128)} %copy-done.8, ...), custom_call_target="tpu_custom_call" | custom-call | flops 402653184 | bytes 1572864 | tf_op jit(solution)/shard_map/pallas_call | solution.py:343
  144.9 2.0 %shard_map.120 = (f32[4,256]{1,0:T(4,128)S(1)}, bf16[4,256,256]{2,1,0:T(8,128)(2,1)S(1)}, bf16[4,256,256]{2,1,0:T(8,128)(2,1)S(1)}, f32[256,256]{1,0:T(8,128)S(1...) custom-call(f32[8,256,256]{2,1,0:T(8,128)} %left.15, f32[8,512,256]{2,1,0:T(8,128)} %right.15, ...), custom_call_target="tpu_custom_call" | custom-call | flops 402653184 | bytes 1572864 | tf_op jit(solution)/shard_map/pallas_call | solution.py:428
  148.9 1.9 %collective-permute-start.24 = (f32[2,256]{1,0:T(2,128)S(1)}, f32[2,256]{1,0:T(2,128)S(1)}, u32[]{:S(2)}, u32[]{:S(2)}) collective-permute-start(f32[2,256]{1,0:T(2,128)S(1)} %get-tuple-element.48), channel_id=1, source_target_pairs={{0,96},{32,0},{64,32},{96,64},{128,224},{160,128},{192,160},{224,1... | collective-permute-start | bytes 6152 | tf_op jit(solution)/shard_map/ppermute | solution.py:447
  152.9 2.9 %collective-permute-done.25.refs_2_ = f32[2,256]{1,0:T(2,128)S(1)} collective-permute-done((f32[2,256]{1,0:T(2,128)S(1)}, f32[2,256]{1,0:T(2,128)S(1)}, u32[]{:S(2)}, u32[]{:S(2)}) %collective-permute-start.25) | collective-permute-done | bytes 2080 | tf_op jit(solution)/shard_map/ppermute | solution.py:447
  (80 shorter events, 17.7 us)
Async XLA Ops:
  3.3 43.1 %collective-permute-start.11 = (f32[384,256]{1,0:T(8,128)S(1)}, f32[384,256]{1,0:T(8,128)S(1)}, u32[]{:S(2)}, u32[]{:S(2)}) collective-permute-start(f32[384,256]{1,0:T(8,128)S(1)} %get-tuple-element.32), channel_id=1, source_target_pairs={{0,32},{32,64},{64,96},{96,0},{128,160},{160,192},{192,224},{224,1... | collective-permute-start | bytes 1179656 | tf_op jit(solution)/shard_map/ppermute | solution.py:315
  7.6 21.9 %collective-permute-start.3 = (f32[128,256]{1,0:T(8,128)S(1)}, f32[128,256]{1,0:T(8,128)S(1)}, u32[]{:S(2)}, u32[]{:S(2)}) collective-permute-start(f32[128,256]{1,0:T(8,128)S(1)} %get-tuple-element.28), channel_id=1, source_target_pairs={{0,32},{32,64},{64,96},{96,0},{128,160},{160,192},{192,224},{224,1... | collective-permute-start | bytes 393224 | tf_op jit(solution)/shard_map/ppermute | solution.py:315
  9.2 37.1 %collective-permute-start.12 = (f32[384,256]{1,0:T(8,128)S(1)}, f32[384,256]{1,0:T(8,128)S(1)}, u32[]{:S(2)}, u32[]{:S(2)}) collective-permute-start(f32[384,256]{1,0:T(8,128)S(1)} %get-tuple-element.33), channel_id=1, source_target_pairs={{0,64},{32,96},{64,0},{96,32},{128,192},{160,224},{192,128},{224,1... | collective-permute-start | bytes 1179656 | tf_op jit(solution)/shard_map/ppermute | solution.py:315
  10.9 20.7 %collective-permute-start.4 = (f32[128,256]{1,0:T(8,128)S(1)}, f32[128,256]{1,0:T(8,128)S(1)}, u32[]{:S(2)}, u32[]{:S(2)}) collective-permute-start(f32[128,256]{1,0:T(8,128)S(1)} %get-tuple-element.29), channel_id=1, source_target_pairs={{0,64},{32,96},{64,0},{96,32},{128,192},{160,224},{192,128},{224,1... | collective-permute-start | bytes 393224 | tf_op jit(solution)/shard_map/ppermute | solution.py:315
  12.7 19.7 %collective-permute-start.16 = (f32[128,256]{1,0:T(8,128)S(1)}, f32[128,256]{1,0:T(8,128)S(1)}, u32[]{:S(2)}, u32[]{:S(2)}) collective-permute-start(f32[128,256]{1,0:T(8,128)S(1)} %get-tuple-element.35), channel_id=1, source_target_pairs={{0,32},{32,64},{64,96},{96,0},{128,160},{160,192},{192,224},{224,1... | collective-permute-start | bytes 393224 | tf_op jit(solution)/shard_map/ppermute | solution.py:315
  29.6 17.6 %collective-permute-start.13 = (f32[384,256]{1,0:T(8,128)S(1)}, f32[384,256]{1,0:T(8,128)S(1)}, u32[]{:S(2)}, u32[]{:S(2)}) collective-permute-start(f32[384,256]{1,0:T(8,128)S(1)} %get-tuple-element.34), channel_id=1, source_target_pairs={{0,96},{32,0},{64,32},{96,64},{128,224},{160,128},{192,160},{224,1... | collective-permute-start | bytes 1179656 | tf_op jit(solution)/shard_map/ppermute | solution.py:315
  31.6 7.9 %collective-permute-start.17 = (f32[128,256]{1,0:T(8,128)S(1)}, f32[128,256]{1,0:T(8,128)S(1)}, u32[]{:S(2)}, u32[]{:S(2)}) collective-permute-start(f32[128,256]{1,0:T(8,128)S(1)} %get-tuple-element.36), channel_id=1, source_target_pairs={{0,64},{32,96},{64,0},{96,32},{128,192},{160,224},{192,128},{224,1... | collective-permute-start | bytes 393224 | tf_op jit(solution)/shard_map/ppermute | solution.py:315
  32.5 10.5 %collective-permute-start.18 = (f32[128,256]{1,0:T(8,128)S(1)}, f32[128,256]{1,0:T(8,128)S(1)}, u32[]{:S(2)}, u32[]{:S(2)}) collective-permute-start(f32[128,256]{1,0:T(8,128)S(1)} %get-tuple-element.37), channel_id=1, source_target_pairs={{0,96},{32,0},{64,32},{96,64},{128,224},{160,128},{192,160},{224,1... | collective-permute-start | bytes 393224 | tf_op jit(solution)/shard_map/ppermute | solution.py:315
  39.5 21.8 %collective-permute-start = (f32[384,256]{1,0:T(8,128)S(1)}, f32[384,256]{1,0:T(8,128)S(1)}, u32[]{:S(2)}, u32[]{:S(2)}) collective-permute-start(f32[384,256]{1,0:T(8,128)S(1)} %get-tuple-element.25), channel_id=1, source_target_pairs={{0,32},{32,64},{64,96},{96,0},{128,160},{160,192},{192,224},{224,1... | collective-permute-start | bytes 1179656 | tf_op jit(solution)/shard_map/ppermute | solution.py:315
  43.0 18.5 %collective-permute-start.1 = (f32[384,256]{1,0:T(8,128)S(1)}, f32[384,256]{1,0:T(8,128)S(1)}, u32[]{:S(2)}, u32[]{:S(2)}) collective-permute-start(f32[384,256]{1,0:T(8,128)S(1)} %get-tuple-element.26), channel_id=1, source_target_pairs={{0,64},{32,96},{64,0},{96,32},{128,192},{160,224},{192,128},{224,1... | collective-permute-start | bytes 1179656 | tf_op jit(solution)/shard_map/ppermute | solution.py:315
  46.3 18.9 %collective-permute-start.2 = (f32[384,256]{1,0:T(8,128)S(1)}, f32[384,256]{1,0:T(8,128)S(1)}, u32[]{:S(2)}, u32[]{:S(2)}) collective-permute-start(f32[384,256]{1,0:T(8,128)S(1)} %get-tuple-element.27), channel_id=1, source_target_pairs={{0,96},{32,0},{64,32},{96,64},{128,224},{160,128},{192,160},{224,1... | collective-permute-start | bytes 1179656 | tf_op jit(solution)/shard_map/ppermute | solution.py:315
  46.3 14.9 %collective-permute-start.5 = (f32[128,256]{1,0:T(8,128)S(1)}, f32[128,256]{1,0:T(8,128)S(1)}, u32[]{:S(2)}, u32[]{:S(2)}) collective-permute-start(f32[128,256]{1,0:T(8,128)S(1)} %get-tuple-element.30), channel_id=1, source_target_pairs={{0,96},{32,0},{64,32},{96,64},{128,224},{160,128},{192,160},{224,1... | collective-permute-start | bytes 393224 | tf_op jit(solution)/shard_map/ppermute | solution.py:315
  47.1 18.5 %collective-permute-start.19 = (f32[3,128,256]{2,1,0:T(8,128)S(1)}, f32[3,128,256]{2,1,0:T(8,128)S(1)}, u32[]{:S(2)}, u32[]{:S(2)}) collective-permute-start(f32[3,128,256]{2,1,0:T(8,128)S(1)} %shard_map.116.refs_3_), channel_id=1, source_target_pairs={{0,1},{1,0},{2,3},{3,2},{4,5},{5,4},{6,7},{7,6},{8,9},{9,8},{10,11... | collective-permute-start | bytes 1179656 | tf_op jit(solution)/shard_map/ppermute | solution.py:315
  61.3 14.9 %collective-permute-start.8 = (f32[256,512]{1,0:T(8,128)S(1)}, f32[256,512]{1,0:T(8,128)S(1)}, u32[]{:S(2)}, u32[]{:S(2)}) collective-permute-start(f32[256,512]{1,0:T(8,128)S(1)} %get-tuple-element.24._.mixed), channel_id=1, source_target_pairs={{2,0},{0,2},{6,4},{4,6},{10,8},{8,10},{14,12},{12,14},{18,16},{16,... | collective-permute-start | bytes 1572872 | tf_op jit(solution)/shard_map/ppermute | solution.py:315
  61.5 54.4 %collective-permute-start.9 = (f32[256,512]{1,0:T(8,128)S(1)}, f32[256,512]{1,0:T(8,128)S(1)}, u32[]{:S(2)}, u32[]{:S(2)}) collective-permute-start(f32[256,512]{1,0:T(8,128)S(1)} %get-tuple-element.24._.mixed), channel_id=1, source_target_pairs={{30,0},{4,2},{2,4},{8,6},{6,8},{12,10},{10,12},{16,14},{14,16},{20... | collective-permute-start | bytes 1572872 | tf_op jit(solution)/shard_map/ppermute | solution.py:315
  65.2 65.7 %collective-permute-start.10 = (f32[256,512]{1,0:T(8,128)S(1)}, f32[256,512]{1,0:T(8,128)S(1)}, u32[]{:S(2)}, u32[]{:S(2)}) collective-permute-start(f32[256,512]{1,0:T(8,128)S(1)} %get-tuple-element.24._.mixed), channel_id=1, source_target_pairs={{16,0},{18,2},{20,4},{22,6},{24,8},{26,10},{28,12},{30,14},{0,16},... | collective-permute-start | bytes 1572872 | tf_op jit(solution)/shard_map/ppermute | solution.py:315
  65.6 66.6 %collective-permute-start.6 = (f32[3,128,256]{2,1,0:T(8,128)S(1)}, f32[3,128,256]{2,1,0:T(8,128)S(1)}, u32[]{:S(2)}, u32[]{:S(2)}) collective-permute-start(f32[3,128,256]{2,1,0:T(8,128)S(1)} %shard_map.106.refs_3_), channel_id=1, source_target_pairs={{0,1},{1,0},{2,3},{3,2},{4,5},{5,4},{6,7},{7,6},{8,9},{9,8},{10,11... | collective-permute-start | bytes 1179656 | tf_op jit(solution)/shard_map/ppermute | solution.py:315
  65.9 68.8 %collective-permute-start.7 = (f32[3,128,256]{2,1,0:T(8,128)S(1)}, f32[3,128,256]{2,1,0:T(8,128)S(1)}, u32[]{:S(2)}, u32[]{:S(2)}) collective-permute-start(f32[3,128,256]{2,1,0:T(8,128)S(1)} %shard_map.107.refs_3_), channel_id=1, source_target_pairs={{0,1},{1,0},{2,3},{3,2},{4,5},{5,4},{6,7},{7,6},{8,9},{9,8},{10,11... | collective-permute-start | bytes 1179656 | tf_op jit(solution)/shard_map/ppermute | solution.py:315
  76.2 65.1 %collective-permute-start.20 = (f32[256,256]{1,0:T(8,128)S(1)}, f32[256,256]{1,0:T(8,128)S(1)}, u32[]{:S(2)}, u32[]{:S(2)}) collective-permute-start(f32[256,256]{1,0:T(8,128)S(1)} %shard_map.118.refs_10_), channel_id=1, source_target_pairs={{0,128},{32,160},{64,192},{96,224},{128,0},{160,32},{192,64},{224,... | collective-permute-start | bytes 786440 | tf_op jit(solution)/shard_map/ppermute | solution.py:315
  115.9 25.4 %collective-permute-start.15 = (f32[256,256]{1,0:T(8,128)S(1)}, f32[256,256]{1,0:T(8,128)S(1)}, u32[]{:S(2)}, u32[]{:S(2)}) collective-permute-start(f32[256,256]{1,0:T(8,128)S(1)} %shard_map.115.refs_9_), channel_id=1, source_target_pairs={{0,128},{32,160},{64,192},{96,224},{128,0},{160,32},{192,64},{224,... | collective-permute-start | bytes 786440 | tf_op jit(solution)/shard_map/ppermute | solution.py:315
  132.7 12.2 %collective-permute-start.22 = (f32[264,256]{1,0:T(8,128)S(1)}, f32[264,256]{1,0:T(8,128)S(1)}, u32[]{:S(2)}, u32[]{:S(2)}) collective-permute-start(f32[264,256]{1,0:T(8,128)S(1)} %shard_map.110.refs_8_), channel_id=1, source_target_pairs={{0,128},{32,160},{64,192},{96,224},{128,0},{160,32},{192,64},{224,... | collective-permute-start | bytes 811016 | tf_op jit(solution)/shard_map/ppermute | solution.py:315
  135.3 11.7 %collective-permute-start.21 = (f32[264,256]{1,0:T(8,128)S(1)}, f32[264,256]{1,0:T(8,128)S(1)}, u32[]{:S(2)}, u32[]{:S(2)}) collective-permute-start(f32[264,256]{1,0:T(8,128)S(1)} %shard_map.112.refs_9_), channel_id=1, source_target_pairs={{0,128},{32,160},{64,192},{96,224},{128,0},{160,32},{192,64},{224,... | collective-permute-start | bytes 811016 | tf_op jit(solution)/shard_map/ppermute | solution.py:315
  150.8 5.1 %collective-permute-start.25 = (f32[2,256]{1,0:T(2,128)S(1)}, f32[2,256]{1,0:T(2,128)S(1)}, u32[]{:S(2)}, u32[]{:S(2)}) collective-permute-start(f32[2,256]{1,0:T(2,128)S(1)} %get-tuple-element.47), channel_id=1, source_target_pairs={{0,64},{32,96},{64,0},{96,32},{128,192},{160,224},{192,128},{224,1... | collective-permute-start | bytes 6152 | tf_op jit(solution)/shard_map/ppermute | solution.py:447
  151.6 4.8 %collective-permute-start.26 = (f32[2,256]{1,0:T(2,128)S(1)}, f32[2,256]{1,0:T(2,128)S(1)}, u32[]{:S(2)}, u32[]{:S(2)}) collective-permute-start(f32[2,256]{1,0:T(2,128)S(1)} %get-tuple-element.46), channel_id=1, source_target_pairs={{0,32},{32,64},{64,96},{96,0},{128,160},{160,192},{192,224},{224,1... | collective-permute-start | bytes 6152 | tf_op jit(solution)/shard_map/ppermute | solution.py:447
  (16 other events, 565.4 us)
